TPU v7x, 32 devices: a whole 2x2x4 slice. The times are simulated.
32 devices in a mesh: seq: 8 (over z, x), tp: 4 (over y, core).
Axes of the slice: x: 2, y: 2, z: 4, core: 2. Of those that a mesh axis runs over, the one named last changes fastest.
Arguments:
- byte_states: bfloat16 [4096, 1024], P('seq'), may hold values from -6 to 6
- flags: int32 [4096], P('seq'), may hold values from 0 to 1, as said below
- stretch_owner: int32 [1024, 1], P('seq'), may hold values from 0 to 7; in each aligned block of 128 rows (0 to 127, 128 to 255, ...) at most 32 rows name the same one
- log_decay: float32 [4096, 16], P('seq', 'tp'), may hold values from -2 to 0, as said below
- w_x: bfloat16 [1024, 2048], P(None, 'tp'), may hold values from -0.1875 to 0.1875
- w_z: bfloat16 [1024, 2048], P(None, 'tp'), may hold values from -0.1875 to 0.1875
- w_bc: bfloat16 [1024, 256], replicated, may hold values from -0.1875 to 0.1875
- w_out: bfloat16 [2048, 1024], P('tp'), may hold values from -0.125 to 0.125
- pad_vector: bfloat16 [512], replicated, may hold values from -5 to 5
- w_q: bfloat16 [1536, 1536], P(None, 'tp'), may hold values from -8 to 8
- w_k: bfloat16 [1536, 1536], P(None, 'tp'), may hold values from -8 to 8
- w_v: bfloat16 [1536, 1536], P(None, 'tp'), may hold values from -0.15625 to 0.15625
- w_o: bfloat16 [1536, 1536], P('tp'), may hold values from -0.15625 to 0.15625
Outputs:
- enc_out: bfloat16 [4096, 1024], P('seq', 'tp')
- main_out: bfloat16 [2048, 1536], P('seq')
Inputs may be any that keep to these rules, and one draw needn't show every extreme that they name: `flags`: exactly 128 ones among each aligned block of 512 bytes. `stretch_owner`: in each aligned block of 128 stretches no owner is named more than 32 times. `log_decay`: negative.
All inputs are finite; a program needn't handle non-finite values.
Results may differ from a plain program's by a relative error of at most 0.015.
Values may be sent and summed in bfloat16 or wider, within the bound.
A program may use at most 128 MiB of HBM per device.

v0:
```python
import math

import jax
import jax.numpy as jnp
from jax import lax
from jax.sharding import PartitionSpec as P

HD = 128
BLOCK = 256


eps = 1e-05
highest = lax.Precision.HIGHEST
far_query = 536870912
far_key = 1073741824


def carried_in(shard, axis, combine, identity):
    peers, index = (lax.axis_size(axis), lax.axis_index(axis))
    everything = jax.tree.map(
        lambda part, kind: lax.all_gather(part.astype(kind), axis),
        shard,
        (jnp.bfloat16, jnp.bfloat16),
    )
    start = jax.tree.map(
        lambda part, zero: jnp.broadcast_to(jnp.asarray(zero, part.dtype), part.shape),
        shard,
        identity,
    )

    def carried_step(k, before):
        reached = k < index
        new = combine(
            before, jax.tree.map(lambda part, own: part[k].astype(own.dtype), everything, shard)
        )
        return jax.tree.map(lambda a, b: jnp.where(reached, a, b), new, before)

    return lax.fori_loop(0, peers, carried_step, start)


def shortened(shard):

    def short(part):
        return part.astype(jnp.bfloat16) if part.dtype == jnp.float32 else part

    return jax.tree.map(short, shard)


def rms_rows(values):
    wide = values.astype(jnp.float32)
    return wide * lax.rsqrt(jnp.mean(wide * wide, axis=-1, keepdims=True) + eps)


def ssd_blocks(xh, bmat, cmat, decay, start_state):
    rows, heads, width_p = xh.shape
    nblk = rows // BLOCK

    def advance(state, block):
        x_blk, b_blk, c_blk, a_blk = block
        cum = jnp.cumsum(a_blk, axis=0)
        later = lax.broadcasted_iota(jnp.int32, (BLOCK, BLOCK), 0)
        earlier = lax.broadcasted_iota(jnp.int32, (BLOCK, BLOCK), 1)
        causal = (later >= earlier)[:, :, None]
        spans = jnp.where(causal, cum[:, None, :] - cum[None, :, :], -1e30)
        intersection = jnp.dot(c_blk, b_blk.T, preferred_element_type=jnp.float32)
        mixing = intersection[:, :, None] * jnp.exp(spans)
        x_wide = x_blk.astype(jnp.float32)
        inside = jnp.einsum("tsh,shp->thp", mixing, x_wide, precision=highest)
        carried = (
            jnp.einsum("tn,hnp->thp", c_blk.astype(jnp.float32), state, precision=highest)
            * jnp.exp(cum)[:, :, None]
        )
        tail = jnp.exp(cum[-1][None, :] - cum)
        fresh = jnp.einsum(
            "sh,sn,shp->hnp", tail, b_blk.astype(jnp.float32), x_wide, precision=highest
        )
        new_state = state * jnp.exp(cum[-1])[:, None, None] + fresh
        return (new_state, inside + carried)

    blocks = (
        xh.reshape(nblk, BLOCK, heads, width_p),
        bmat.reshape(nblk, BLOCK, -1),
        cmat.reshape(nblk, BLOCK, -1),
        decay.reshape(nblk, BLOCK, heads),
    )
    final, outs = lax.scan(advance, start_state, blocks)
    return (outs.reshape(rows, heads, width_p), final)


def link_states(earlier, later):
    return (earlier[0] + later[0], earlier[1] * jnp.exp(later[0])[..., None, None] + later[1])


def attend_block(carry, queries, query_pos, key_blk, value_blk, key_pos, scale):
    best, total, accum = carry
    scores = (
        jnp.einsum("qhd,khd->hqk", queries, key_blk, preferred_element_type=jnp.float32) * scale
    )
    allowed = key_pos[None, None, :] <= query_pos[None, :, None]
    scores = jnp.where(allowed, scores, -1e30)
    new_best = jnp.maximum(best, jnp.max(scores, axis=2))
    shrink = jnp.exp(best - new_best)
    expo = jnp.where(allowed, jnp.exp(scores - new_best[:, :, None]), 0.0)
    total = total * shrink + jnp.sum(expo, axis=2)
    accum = accum * jnp.transpose(shrink)[:, :, None] + jnp.einsum(
        "hqk,khd->qhd", expo.astype(jnp.bfloat16), value_blk, preferred_element_type=jnp.float32
    )
    return (new_best, total, accum)


def on_device(
    byte_states,
    flags,
    stretch_owner,
    log_decay,
    w_x,
    w_z,
    w_bc,
    w_out,
    pad_vector,
    w_q,
    w_k,
    w_v,
    w_o,
):
    rows, width = byte_states.shape
    heads_here = log_decay.shape[1]
    head_p = w_x.shape[1] // heads_here
    state_n = w_bc.shape[1] // 2
    ranks = lax.axis_size("seq")
    split_tp = lax.axis_size("tp")
    normed = rms_rows(byte_states).astype(jnp.bfloat16)
    xs = jnp.dot(normed, w_x, preferred_element_type=jnp.float32).astype(jnp.bfloat16)
    zgate = jnp.dot(normed, w_z, preferred_element_type=jnp.float32)
    projected = jnp.dot(normed, w_bc, preferred_element_type=jnp.float32).astype(jnp.bfloat16)
    bmat = projected[:, :state_n]
    cmat = projected[:, state_n:]
    start_state = jnp.zeros((heads_here, state_n, head_p), jnp.float32)
    local_mixed, final = ssd_blocks(
        xs.reshape(rows, heads_here, head_p), bmat, cmat, log_decay, start_state
    )
    running = jnp.cumsum(log_decay, axis=0)
    identity = (jnp.zeros((heads_here,), jnp.float32), jnp.zeros_like(final))
    carried = carried_in((running[-1], final), "seq", link_states, identity)
    incoming = carried[1]
    mixed = (
        local_mixed
        + jnp.einsum("tn,hnp->thp", cmat.astype(jnp.float32), incoming, precision=highest)
        * jnp.exp(running)[:, :, None]
    )
    gated = mixed * jax.nn.silu(zgate).reshape(rows, heads_here, head_p)
    scaled = gated * lax.rsqrt(jnp.mean(gated * gated, axis=2, keepdims=True) + eps)
    scaled = scaled.reshape(rows, heads_here * head_p).astype(jnp.bfloat16)
    partial_enc = jnp.dot(scaled, w_out, preferred_element_type=jnp.float32)
    quarter = width // split_tp
    column_start = lax.axis_index("tp") * quarter
    stretches_here = stretch_owner.shape[0]
    flag_rank = jnp.cumsum(flags) - 1
    stretch_ids = lax.broadcasted_iota(jnp.int32, (stretches_here, rows), 0)
    picker = ((flag_rank[None, :] == stretch_ids) & (flags[None, :] == 1)).astype(jnp.bfloat16)
    summed = lax.psum(partial_enc.astype(jnp.bfloat16), "tp").astype(jnp.float32)
    encoded = (byte_states.astype(jnp.float32) + summed).astype(jnp.bfloat16)
    enc_out = lax.dynamic_slice_in_dim(encoded, column_start, quarter, 1)
    stretch_rows = jnp.dot(picker, encoded, preferred_element_type=jnp.float32).astype(jnp.bfloat16)
    cap = max(2, 2 * stretches_here // ranks)
    slots = ranks * cap
    owners = stretch_owner[:, 0]
    owner_hot = (
        owners[:, None] == lax.broadcasted_iota(jnp.int32, (stretches_here, ranks), 1)
    ).astype(jnp.int32)
    before = jnp.cumsum(owner_hot, axis=0) - owner_hot
    order = jnp.sum(before * owner_hot, axis=1)
    slot = owners * cap + order
    slot_ids = lax.broadcasted_iota(jnp.int32, (slots, stretches_here), 0)
    placed = slot_ids == slot[None, :]
    anchor = lax.axis_index("seq") * stretches_here + lax.broadcasted_iota(
        jnp.int32, (stretches_here,), 0
    )
    send_pos = jnp.where(
        jnp.any(placed, axis=1), jnp.sum(jnp.where(placed, anchor[None, :], 0), axis=1), -1
    )
    send_rows = jnp.dot(
        placed.astype(jnp.bfloat16), stretch_rows, preferred_element_type=jnp.float32
    ).astype(jnp.bfloat16)
    got_rows, got_pos = (
        lax.all_to_all(
            send_rows.reshape(ranks, cap, width), "seq", split_axis=0, concat_axis=0, tiled=True
        ),
        lax.all_to_all(
            send_pos.reshape(ranks, cap), "seq", split_axis=0, concat_axis=0, tiled=True
        ),
    )
    got_rows = got_rows.reshape(slots, width)
    got_pos = got_pos.reshape(slots)
    valid = got_pos >= 0
    padding = jnp.where(valid[:, None], pad_vector[None, :], jnp.zeros((), jnp.bfloat16))
    stream = jnp.concatenate([got_rows, padding], axis=1)
    stream_norm = rms_rows(stream).astype(jnp.bfloat16)
    heads_main = w_q.shape[1] // HD
    scale = 1.0 / math.sqrt(HD)
    queries = (
        jnp.dot(stream_norm, w_q, preferred_element_type=jnp.float32)
        .astype(jnp.bfloat16)
        .reshape(slots, heads_main, HD)
    )
    query_pos = jnp.where(valid, got_pos, far_query)
    start_carry = (
        jnp.full((heads_main, slots), -1e30, jnp.float32),
        jnp.zeros((heads_main, slots), jnp.float32),
        jnp.zeros((slots, heads_main, HD), jnp.float32),
    )
    keys_here = (
        jnp.dot(stream_norm, w_k, preferred_element_type=jnp.float32)
        .astype(jnp.bfloat16)
        .reshape(slots, heads_main, HD)
    )
    values_here = (
        jnp.dot(stream_norm, w_v, preferred_element_type=jnp.float32)
        .astype(jnp.bfloat16)
        .reshape(slots, heads_main, HD)
    )
    key_pos_here = jnp.where(valid, got_pos, far_key)
    key_rows = lax.all_gather(keys_here, "seq", axis=0, tiled=True)
    count = key_rows.shape[0]
    size = math.gcd(count, 512)
    nblk = count // size

    def fold_step(state, block):
        return (attend_block(state, queries, query_pos, block[0], block[1], block[2], scale), None)

    blocks = (
        key_rows.reshape(nblk, size, heads_main, HD),
        lax.all_gather(values_here, "seq", axis=0, tiled=True).reshape(nblk, size, heads_main, HD),
        lax.all_gather(shortened(key_pos_here), "seq", axis=0, tiled=True).reshape(nblk, size),
    )
    best, total, accum = lax.scan(fold_step, start_carry, blocks)[0]
    attended = (
        (accum / jnp.transpose(total)[:, :, None])
        .astype(jnp.bfloat16)
        .reshape(slots, heads_main * HD)
    )
    summed_main = lax.psum(
        jnp.dot(attended, w_o, preferred_element_type=jnp.float32).astype(jnp.bfloat16), "tp"
    ).astype(jnp.float32)
    main_out = jnp.where(valid[:, None], stream.astype(jnp.float32) + summed_main, 0.0).astype(
        jnp.bfloat16
    )
    return (enc_out, main_out)


def solution(mesh):
    placed = (
        P("seq", None),
        P("seq"),
        P("seq", None),
        P("seq", "tp"),
        P(None, "tp"),
        P(None, "tp"),
        P(),
        P("tp", None),
        P(),
        P(None, "tp"),
        P(None, "tp"),
        P(None, "tp"),
        P("tp", None),
    )
    return jax.shard_map(
        on_device,
        mesh=mesh,
        in_specs=placed,
        out_specs=(P("seq", "tp"), P("seq", None)),
        check_vma=False,
    )
```

profile of v0, /device:TPU:0, one launch (start us, length us, event | category | flops | bytes accessed | tf_op | source)
XLA Modules:
  0.0 318.6 jit_solution(18168973310382984664)
XLA Ops:
  7.2 1.6 fusion.45
  8.9 2.0 convolution_convert_fusion.4
  12.5 32.7 %while.42 = (s32[]{:T(128)}, f32[4,128,128]{2,1,0:T(8,128)S(1)}, f32[2,256,4,128]{1,0,3,2:T(2,128)}, f32[2,256,4]{1,2,0:T(4,128)S(1)}, bf16[2,256,128]{2,1,0:T(8...) while((s32[]{:T(128)}, f32[4,128,128]{2,1,0:T(8,128)S(1)}, ...), condition=%wide.region_4.5_spmd.clone, body=%wide.region_1.4_spmd.clone.sunk | while | flops 823755776 | bytes 7013988 | solution.py:86
  12.5 1.2 reduce-window.39
  17.3 11.5 %dynamic_update_slice.6 = f32[2,256,4,128]{1,0,3,2:T(2,128)} dynamic-update-slice(f32[2,256,4,128]{1,0,3,2:T(2,128)} %get-tuple-element.594, f32[1,256,4,128]{1,0,3,2:T(1,128)S(1)} %copy.191, s32[]{:T(128)S(6)} %copy.196, s32[]{:T(128)} %constant.107.clone.1..sunk, s32[]{:T(128)} %constant.107.clone.1..sunk, s32[]{:T(128)} %constant.107.clone.1..sunk) | dynamic-update-slice | bytes 1048580 | tf_op jit(solution)/shard_map/while/body/jit(dynamic_update_index_in_dim)/dynamic_update_slice | solution.py:86
  28.9 1.2 reduce-window.39
  33.7 11.5 %dynamic_update_slice.6 = f32[2,256,4,128]{1,0,3,2:T(2,128)} dynamic-update-slice(f32[2,256,4,128]{1,0,3,2:T(2,128)} %get-tuple-element.594, f32[1,256,4,128]{1,0,3,2:T(1,128)S(1)} %copy.191, s32[]{:T(128)S(6)} %copy.196, s32[]{:T(128)} %constant.107.clone.1..sunk, s32[]{:T(128)} %constant.107.clone.1..sunk, s32[]{:T(128)} %constant.107.clone.1..sunk) | dynamic-update-slice | bytes 1048580 | tf_op jit(solution)/shard_map/while/body/jit(dynamic_update_index_in_dim)/dynamic_update_slice | solution.py:86
  46.0 1.2 reduce-window.23
  49.6 7.3 %all-to-all-start = ((s32[8,1,32]{2,1,0:T(1,128)}), s32[8,1,32]{2,1,0:T(1,128)}, u32[]{:S(2)}, u32[]{:S(2)}) async-start(s32[8,1,32]{2,1,0:T(1,128)} %select_n.72), calls=%async_computation | async-start | bytes 8192 | tf_op jit(solution)/shard_map/all_to_all | solution.py:189
  56.9 21.2 %all-gather.1 = bf16[8,1,4]{2,1,0:T(2,128)(2,1)} all-gather(bf16[1,1,4]{2,1,0:T(2,128)(2,1)S(1)} %slice_bitcast_fusion), channel_id=1, replica_groups=mesh['seq'=8,'tp'=4] {'seq'}, dimensions={0}, use_global_device_ids=true | all-gather | bytes 72 | tf_op jit(solution)/shard_map/all_gather | solution.py:21
  78.1 2.1 reshape.237
  83.3 3.2 %divide_multiply_fusion = f32[512,512]{0,1:T(8,128)} fusion(bf16[1024,512]{1,0:T(8,128)(2,1)} %param.24, bf16[512,1024]{1,0:T(8,128)(2,1)S(1)} %copy-done.5, f32[512]{0:T(512)} %copy-done.16), kind=kOutput, calls=%fused_computation.92 | convolution fusion | flops 539492352 | bytes 3147776 | tf_op jit(solution)/shard_map/dot_general | solution.py:134
  86.6 2.7 all-gather.11.cloned.1.call-done
  89.2 13.7 %while.43 = (s32[]{:T(128)}, f32[4,128,128]{2,1,0:T(8,128)S(1)}, s32[]{:T(128)}, bf16[8,4]{1,0:T(8,128)(2,1)}, bf16[8,4,128,128]{3,2,1,0:T(8,128)(2,1)}, /*index=5*/s32[]{:T(128)}, s32[]{:T(128)}) while((s32[]{:T(128)}, f32[4,128,128]{2,1,0:T(8,128)S(1)}, s32[]{:T(128)}, bf16[8,4]{1,0:T(8,128)(2,1)}, ...), condition=%wide.region_8.9_spmd.clone, body=%wide.region_7.8_spmd.clone.sunk | while | flops 327688 | bytes 655513 | solution.py:38
  91.6 1.0 fusion.115
  93.3 1.0 fusion.115
  96.7 1.0 fusion.115
  101.9 1.0 fusion.115
  103.7 1.7 fusion.62
  106.0 1.1 copy-done.19
  107.1 1.8 convolution_convert_fusion.1
  109.1 34.9 %all-reduce.3.cloned.1.call-done = bf16[512,1024]{1,0:T(8,128)(2,1)} async-done(((bf16[512,1024]{1,0:T(8,128)(2,1)}), bf16[512,1024]{1,0:T(8,128)(2,1)}) %all-reduce.3.cloned.1.call-update) | async-done | bytes 1048592 | tf_op jit(solution)/shard_map/psum | solution.py:161
  144.0 1.6 fusion.47
  145.7 1.3 convolution_convert_fusion.2
  147.0 5.5 %all-to-all-start.1 = ((bf16[8,32,1024]{2,1,0:T(8,128)(2,1)}), bf16[8,32,1024]{2,1,0:T(8,128)(2,1)S(1)}, u32[]{:S(2)}, u32[]{:S(2)}) async-start(bf16[8,32,1024]{2,1,0:T(8,128)(2,1)} %bitcast.182), calls=%async_computation.1 | async-start | bytes 1048576 | tf_op jit(solution)/shard_map/all_to_all | solution.py:186
  153.1 1.3 reduce.10
  154.6 11.8 %all-to-all-done.1 = bf16[8,32,1024]{2,1,0:T(8,128)(2,1)S(1)} async-done(((bf16[8,32,1024]{2,1,0:T(8,128)(2,1)}), bf16[8,32,1024]{2,1,0:T(8,128)(2,1)S(1)}, u32[]{:S(2)}, u32[]{:S(2)}) %all-to-all-start.1) | async-done | bytes 524320 | tf_op jit(solution)/shard_map/all_to_all | solution.py:186
  166.7 1.9 convolution_convert_fusion.8
  169.7 1.9 convolution_convert_fusion.6
  172.5 18.7 %all-gather.2 = s32[8,1,256]{2,1,0:T(1,128)S(1)} all-gather(s32[1,1,256]{2,1,0:T(1,128)S(1)} %bitcast.201), channel_id=1, replica_groups=mesh['seq'=8,'tp'=4] {'seq'}, dimensions={0}, use_global_device_ids=true | all-gather | bytes 9216 | tf_op jit(solution)/shard_map/all_gather | solution.py:234
  191.2 1.9 convolution_convert_fusion.7
  193.4 19.5 %all-gather.7.cloned.1.call-done = bf16[2048,3,128]{0,2,1:T(8,128)(2,1)} async-done(((bf16[256,3,128]{0,2,1:T(8,128)(2,1)}), bf16[2048,3,128]{0,2,1:T(8,128)(2,1)}) %all-gather.7.cloned.1.call-update) | async-done | bytes 1572880 | tf_op jit(solution)/shard_map/all_gather | solution.py:223
  213.0 2.6 copy.141
  215.6 42.5 %all-gather.9.cloned.1.call-done = bf16[2048,3,128]{0,2,1:T(8,128)(2,1)} async-done(((bf16[256,3,128]{0,2,1:T(8,128)(2,1)}), bf16[2048,3,128]{0,2,1:T(8,128)(2,1)}) %all-gather.9.cloned.1.call-update) | async-done | bytes 1572880 | tf_op jit(solution)/shard_map/all_gather | solution.py:233
  258.1 2.6 copy.144
  260.7 14.2 %while.44 = (s32[]{:T(128)}, f32[3,256]{1,0:T(4,128)S(1)}, f32[3,256]{1,0:T(4,128)S(1)}, f32[256,3,128]{0,2,1:T(8,128)S(1)}, s32[4,512]{1,0:T(4,128)S(1)}, /*ind...) while((s32[]{:T(128)}, f32[3,256]{1,0:T(4,128)S(1)}, ...), condition=%wide.region_21.22_spmd.clone, body=%wide.region_18.21_spmd.clone.sunk | while | flops 205296128 | bytes 7068813 | solution.py:236
  260.8 1.4 fusion.119
  262.6 1.6 fusion.123
  264.4 1.4 fusion.119
  266.2 1.6 fusion.123
  267.9 1.4 fusion.119
  269.7 1.6 fusion.123
  271.5 1.4 fusion.119
  273.2 1.6 fusion.123
  274.9 1.5 convolution_convert_fusion
  276.4 1.7 constant_dynamic-slice_fusion.4
  278.1 31.7 %all-reduce.5.cloned.1.call-done = bf16[256,1536]{1,0:T(8,128)(2,1)} async-done(((bf16[256,1536]{1,0:T(8,128)(2,1)}), bf16[256,1536]{1,0:T(8,128)(2,1)}) %all-reduce.5.cloned.1.call-update) | async-done | bytes 786448 | tf_op jit(solution)/shard_map/psum | solution.py:242
  309.8 2.3 fusion.51
  (183 shorter events, 31.3 us)
Async XLA Ops:
  7.2 267.7 %copy-start = (bf16[384,1536]{1,0:T(8,128)(2,1)S(1)}, bf16[384,1536]{1,0:T(8,128)(2,1)}, u32[]{:S(2)}) copy-start(bf16[384,1536]{1,0:T(8,128)(2,1)} %param.31) | copy-start | bytes 3538948
  7.2 82.0 %all-gather.11.cloned.1.call-start = ((), (), s32[]{:S(2)}) async-start(), calls=%async_computation.6 | async-start | bytes 1179648 | tf_op jit(solution)/shard_map/all_gather | solution.py:21
  8.8 2.7 copy-start.4
  8.8 2.7 copy-start.18
  8.9 3.5 %copy-start.16 = (f32[512]{0:T(512)}, f32[512]{0:T(512)S(1)}, u32[]{:S(2)}) copy-start(f32[512]{0:T(512)S(1)} %add_rsqrt_fusion.1) | copy-start | bytes 6148
  10.9 0.7 copy-start.9
  11.6 0.9 copy-start.10
  12.5 35.3 %copy-start.13 = (s32[128,1]{0,1:T(1,128)S(1)}, s32[128,1]{0,1:T(1,128)}, u32[]{:S(2)}) copy-start(s32[128,1]{0,1:T(1,128)} %param.21) | copy-start | bytes 1540
  45.2 38.1 %copy-start.5 = (bf16[512,1024]{1,0:T(8,128)(2,1)S(1)}, bf16[512,1024]{1,0:T(8,128)(2,1)}, u32[]{:S(2)}) copy-start(bf16[512,1024]{1,0:T(8,128)(2,1)} %param.19) | copy-start | bytes 3145732
  48.3 0.5 copy-start.14
  49.6 97.4 %all-to-all-start = ((s32[8,1,32]{2,1,0:T(1,128)}), s32[8,1,32]{2,1,0:T(1,128)}, u32[]{:S(2)}, u32[]{:S(2)}) async-start(s32[8,1,32]{2,1,0:T(1,128)} %select_n.72), calls=%async_computation | async-start | bytes 8192 | tf_op jit(solution)/shard_map/all_to_all | solution.py:189
  56.9 87.2 %all-reduce.3.cloned.1.call-start = ((), (), s32[]{:S(2)}) async-start(), calls=%async_computation.2 | async-start | bytes 2097152 | tf_op jit(solution)/shard_map/psum | solution.py:161
  103.7 1.7 copy-start.8
  105.9 1.2 copy-start.19
  107.1 1.8 copy-start.11
  107.1 1.9 copy-start.12
  109.1 36.6 %copy-start.15 = (s32[128]{0:T(128)S(1)}, s32[128]{0:T(128)}, u32[]{:S(2)}) copy-start(s32[128]{0:T(128)} %copy-done.14) | copy-start | bytes 1540
  145.7 21.0 %copy-start.1 = (bf16[512,1024]{1,0:T(8,128)(2,1)}, bf16[512,1024]{1,0:T(8,128)(2,1)S(1)}, u32[]{:S(2)}) copy-start(bf16[512,1024]{1,0:T(8,128)(2,1)S(1)} %fusion.47) | copy-start | bytes 3145732
  145.7 8.8 %copy-start.17 = (bf16[512]{0:T(512)(128)(2,1)S(1)}, bf16[512]{0:T(512)(128)(2,1)}, u32[]{:S(2)}) copy-start(bf16[512]{0:T(512)(128)(2,1)} %param.27) | copy-start | bytes 3076
  147.0 19.5 %all-to-all-start.1 = ((bf16[8,32,1024]{2,1,0:T(8,128)(2,1)}), bf16[8,32,1024]{2,1,0:T(8,128)(2,1)S(1)}, u32[]{:S(2)}, u32[]{:S(2)}) async-start(bf16[8,32,1024]{2,1,0:T(8,128)(2,1)} %bitcast.182), calls=%async_computation.1 | async-start | bytes 1048576 | tf_op jit(solution)/shard_map/all_to_all | solution.py:186
  152.5 60.5 %all-gather.7.cloned.1.call-start = ((), (), s32[]{:S(2)}) async-start(), calls=%async_computation.3 | async-start | bytes 1769472 | tf_op jit(solution)/shard_map/all_gather | solution.py:223
  154.6 36.6 %copy-start.6 = (bf16[256,512]{1,0:T(8,128)(2,1)}, bf16[256,512]{1,0:T(8,128)(2,1)S(1)}, u32[]{:S(2)}) copy-start(bf16[256,512]{1,0:T(8,128)(2,1)S(1)} %broadcast_select_fusion) | copy-start | bytes 786436
  166.5 24.8 %copy-start.2 = (bf16[8,32,1024]{2,1,0:T(8,128)(2,1)}, bf16[8,32,1024]{2,1,0:T(8,128)(2,1)S(1)}, u32[]{:S(2)}) copy-start(bf16[8,32,1024]{2,1,0:T(8,128)(2,1)S(1)} %all-to-all-done.1) | copy-start | bytes 1572868
  169.5 88.6 %all-gather.9.cloned.1.call-start = ((), (), s32[]{:S(2)}) async-start(), calls=%async_computation.4 | async-start | bytes 1769472 | tf_op jit(solution)/shard_map/all_gather | solution.py:233
  172.4 137.4 %all-reduce.5.cloned.1.call-start = ((), (), s32[]{:S(2)}) async-start(), calls=%async_computation.5 | async-start | bytes 1572864 | tf_op jit(solution)/shard_map/psum | solution.py:242
  274.9 34.9 %copy-start.3 = (bf16[8,32,1024]{2,1,0:T(8,128)(2,1)S(1)}, bf16[8,32,1024]{2,1,0:T(8,128)(2,1)}, u32[]{:S(2)}) copy-start(bf16[8,32,1024]{2,1,0:T(8,128)(2,1)} %copy-done.2) | copy-start | bytes 1572868
  274.9 34.9 %copy-start.7 = (bf16[256,512]{1,0:T(8,128)(2,1)S(1)}, bf16[256,512]{1,0:T(8,128)(2,1)}, u32[]{:S(2)}) copy-start(bf16[256,512]{1,0:T(8,128)(2,1)} %copy-done.6) | copy-start | bytes 786436
Sparse Core Ops, SparseCore 0:
  46.1 43.1 all-gather.10
  109.0 34.9 all-reduce.2
  169.6 43.3 all-gather.6
  215.4 42.5 all-gather.8
  276.5 33.2 all-reduce.4
where the time goes:
time: 321 us; the launch traced here: 319 us
  waiting for transfers between devices  143 us (45%)
  local copies, waits for them, and re-layouts  43 us (13%)
  blocking collectives  39.8 us (12%)
  matrix products  33.9 us (11%)
  other arithmetic  30.7 us (10%)
  between operations  14.2 us (4%)
  starting transfers between devices  13.2 us (4%)
    all_gather x1, waiting for transfers between devices, on_device(): lax.all_gather(values_here, 'seq', axis=0, tiled=True)  42.5 us
    psum x1, waiting for transfers between devices, on_device(): lax.psum(partial_enc.astype(jnp.bfloat16), 'tp').astype(jnp.float32)  34.9 us
    psum x1, waiting for transfers between devices, on_device(): lax.psum(jnp.dot(attended, w_o, preferred_element_type=jnp.float32).astyp...  31.7 us
    dynamic_update_slice x4, local copies, waits for them, and re-layouts, ssd_blocks(): final, outs = lax.scan(advance, start_state, blocks)  24.1 us
    all_gather x1, blocking collectives, carried_in(): lax.all_gather(part.astype(kind), axis)  21.2 us
    all_gather x1, waiting for transfers between devices, on_device(): key_rows = lax.all_gather(keys_here, 'seq', axis=0, tiled=True)  19.5 us
    all_gather x1, blocking collectives, on_device(): lax.all_gather(shortened(key_pos_here), 'seq', axis=0, tiled=True)  18.7 us
    all_to_all x1, waiting for transfers between devices, on_device(): lax.all_to_all(send_rows.reshape(ranks, cap, width), 'seq', split_axis=0,...  11.8 us
  transfers between devices with their start and end apart: 7, of which 6 were waited for; matrix products, arithmetic and copies ran while one was open for 14% of the time, Pallas kernels for 0%

commit v1 on v0

v1 whole, which is shorter than its diff:
```python
import functools
import math

import jax
import jax.numpy as jnp
from jax import lax
from jax.experimental import pallas as pl
from jax.experimental.pallas import tpu as pltpu
from jax.sharding import PartitionSpec as P

HD = 128
eps = 1e-05
f32 = jnp.float32
bf16 = jnp.bfloat16
MESH = pl.DeviceIdType.MESH
VM = pl.BlockSpec(memory_space=pltpu.VMEM)
DMA = pltpu.SemaphoreType.DMA


def mm(a, b):
    return jnp.dot(a, b, preferred_element_type=f32)


def mm_t(a, b):
    return lax.dot_general(a, b, (((1,), (1,)), ((), ())), preferred_element_type=f32)


def t_mm(a, b):
    return lax.dot_general(a, b, (((0,), (0,)), ((), ())), preferred_element_type=f32)


def three(a):
    hi = a.astype(bf16)
    rest = a - hi.astype(f32)
    mid = rest.astype(bf16)
    low = (rest - mid.astype(f32)).astype(bf16)
    return hi, mid, low


def iota(shape, dim):
    return lax.broadcasted_iota(jnp.int32, shape, dim)


def local_kernel(
    bytes_ref, wx_ref, wz_ref, wbc_ref, decay_ref, mixed_ref, gate_ref, c_ref, grow_ref, state_ref
):
    rows = bytes_ref.shape[0]
    heads = decay_ref.shape[1]
    state_n = wbc_ref.shape[1] // 2
    p = wx_ref.shape[1] // heads
    wide = bytes_ref[...].astype(f32)
    normed = (wide * lax.rsqrt(jnp.mean(wide * wide, axis=-1, keepdims=True) + eps)).astype(bf16)
    bc = mm(normed, wbc_ref[...]).astype(bf16)
    bmat, cmat = bc[:, :state_n], bc[:, state_n:]
    c_ref[...] = cmat
    xs = mm(normed, wx_ref[...]).astype(bf16)
    parts = three(decay_ref[...])
    lower = (iota((rows, rows), 0) >= iota((rows, rows), 1)).astype(f32).astype(bf16)
    upper = (iota((rows, rows), 0) <= iota((rows, rows), 1)).astype(f32).astype(bf16)
    ones = jnp.ones((rows, state_n), bf16)
    cum = sum(mm(lower, part) for part in parts)
    cum_row = sum(t_mm(part, upper) for part in parts)
    total = sum(t_mm(part, ones) for part in parts)
    last = cum[rows - 1 : rows, :]
    grow_ref[...] = jnp.exp(cum)
    tail = jnp.exp(last - cum)
    for h in range(heads):
        scaled = (xs[:, h * p : (h + 1) * p].astype(f32) * tail[:, h : h + 1]).astype(bf16)
        state_ref[h * state_n : (h + 1) * state_n, :] = t_mm(bmat, scaled).astype(bf16)
    pieces = [piece.astype(f32) for piece in three(total)]
    filler = jnp.zeros((16 - heads % 16, state_n), f32)
    for i, piece in enumerate(pieces):
        start = heads * state_n + 16 * i
        state_ref[start : start + 16, :] = jnp.concatenate([piece, filler], axis=0).astype(bf16)
    z = mm(normed, wz_ref[...])
    gate_ref[...] = z * jax.nn.sigmoid(z)
    half = rows // 2
    for r in range(2):
        lo, hi = r * half, (r + 1) * half
        inter = mm_t(cmat[lo:hi], bmat[:hi])
        causal = iota((half, hi), 0) + lo >= iota((half, hi), 1)
        for h in range(heads):
            spans = cum[lo:hi, h : h + 1] - cum_row[h : h + 1, :hi]
            mixing = (inter * jnp.exp(jnp.where(causal, spans, -1e30))).astype(bf16)
            mixed_ref[lo:hi, h * p : (h + 1) * p] = mm(mixing, xs[:hi, h * p : (h + 1) * p])


def encode_kernel(
    split, every_ref, mixed_ref, gate_ref, c_ref, grow_ref, wout_ref, flags_ref, bytes_ref,
    part_ref, rows_ref, base_ref,
):
    me = lax.axis_index("seq")
    rows, heads = grow_ref.shape
    state_n = c_ref.shape[1]
    p = mixed_ref.shape[1] // heads
    cmat = c_ref[...]
    scaled = []

    def step(k, state):
        block = every_ref[k].astype(f32)
        size = heads * state_n
        total = block[size : size + 16] + block[size + 16 : size + 32] + block[size + 32 :]
        shrink = jnp.exp(total)
        return tuple(
            state[h] * shrink[h : h + 1] + block[h * state_n : (h + 1) * state_n]
            for h in range(heads)
        )

    state = lax.fori_loop(
        0, me, step, tuple(jnp.zeros((state_n, p), f32) for _ in range(heads))
    )
    for h in range(heads):
        cols = slice(h * p, (h + 1) * p)
        mixed = mixed_ref[:, cols] + mm(cmat, state[h].astype(bf16)) * grow_ref[:, h : h + 1]
        gated = mixed * gate_ref[:, cols]
        norm = lax.rsqrt(jnp.mean(gated * gated, axis=1, keepdims=True) + eps)
        scaled.append((gated * norm).astype(bf16))
    scaled = jnp.concatenate(scaled, axis=1)
    count = rows_ref.shape[1]
    flags = flags_ref[...]
    upper = (iota((rows, rows), 0) <= iota((rows, rows), 1)).astype(f32).astype(bf16)
    many = jnp.broadcast_to(flags.astype(f32), (16, rows)).astype(bf16)
    rank = mm(many, upper)[0:1, :].astype(jnp.int32) - 1
    hit = (rank == iota((count, rows), 0)) & (flags == 1)
    picker = jnp.where(hit, 1.0, 0.0).astype(bf16)
    base_ref[...] = mm(picker, bytes_ref[...]).astype(bf16)
    quarter = wout_ref.shape[1] // split
    for q in range(split):
        part = mm(scaled, wout_ref[:, q * quarter : (q + 1) * quarter]).astype(bf16)
        part_ref[q] = part
        rows_ref[q] = mm(picker, part).astype(bf16)


def project_kernel(rows_ref, pad_ref, wq_ref, wk_ref, wv_ref, owner_ref, q_ref, kv_ref, stream_ref, place_ref):
    split, count, quarter = rows_ref.shape
    pad = jnp.broadcast_to(pad_ref[...].astype(f32), (count, pad_ref.shape[1])).astype(bf16)
    stream = jnp.concatenate([rows_ref[q] for q in range(split)] + [pad], axis=1)
    size = stream.shape[1] // split
    for q in range(split):
        stream_ref[q] = stream[:, q * size : (q + 1) * size]
    wide = stream.astype(f32)
    norm = (wide * lax.rsqrt(jnp.mean(wide * wide, axis=-1, keepdims=True) + eps)).astype(bf16)
    q_ref[...] = mm(norm, wq_ref[...]).astype(bf16)
    width = wk_ref.shape[1]
    kv_ref[:, :width] = mm(norm, wk_ref[...]).astype(bf16)
    kv_ref[:, width:] = mm(norm, wv_ref[...]).astype(bf16)
    slots = place_ref.shape[1]
    owner = owner_ref[...]
    ranks = -(-lax.axis_size("seq") // 128) * 128
    hot = jnp.where(owner == iota((count, ranks), 1), 1.0, 0.0)
    strict = jnp.where(iota((count, count), 0) > iota((count, count), 1), 1.0, 0.0)
    before = mm(strict.astype(bf16), hot.astype(bf16))
    order = jnp.sum(before * hot, axis=1, keepdims=True).astype(jnp.int32)
    cap = slots // lax.axis_size("seq")
    slot = owner * cap + order
    place_ref[...] = jnp.where(slot == iota((count, slots), 1), 1.0, 0.0).astype(bf16)


def attend_kernel(group, split, q_ref, all_ref, wo_ref, out_ref):
    me = lax.axis_index("seq")
    ranks, count, width2 = all_ref.shape
    width = width2 // 2
    heads = width // HD
    scale = 1.0 / math.sqrt(HD)
    keys = group * count

    def chunk(c, carry):
        start = c * group
        blocks = all_ref[pl.ds(start, group)]
        blocks = blocks.reshape(keys, width2)
        key_pos = start * count + iota((count, keys), 1)
        allowed = key_pos <= me * count + iota((count, keys), 0)
        seen = start * count + iota((keys, width), 0) < (me + 1) * count
        values = jnp.where(seen, blocks[:, width:], jnp.zeros((), bf16))
        new = []
        for h in range(heads):
            best, total, accum = carry[h]
            cols = slice(h * HD, (h + 1) * HD)
            scores = mm_t(q_ref[:, cols], blocks[:, cols]) * scale
            scores = jnp.where(allowed, scores, -1e30)
            top = jnp.maximum(best, jnp.max(scores, axis=1, keepdims=True))
            shrink = jnp.exp(best - top)
            expo = jnp.exp(scores - top)
            total = total * shrink + jnp.sum(expo, axis=1, keepdims=True)
            accum = accum * shrink + mm(expo.astype(bf16), values[:, cols])
            new.append((top, total, accum))
        return tuple(new)

    start = tuple(
        (jnp.full((count, 1), -1e30, f32), jnp.zeros((count, 1), f32), jnp.zeros((count, HD), f32))
        for _ in range(heads)
    )
    if ranks == group:
        done = chunk(0, start)
    else:
        done = lax.fori_loop(0, me // group + 1, chunk, start)
    attended = jnp.concatenate([(a / t).astype(bf16) for _, t, a in done], axis=1)
    size = wo_ref.shape[1] // split
    for q in range(split):
        out_ref[q] = mm(attended, wo_ref[:, q * size : (q + 1) * size]).astype(bf16)


def greet(devices):
    barrier = pltpu.get_barrier_semaphore()
    for device in devices:
        pl.semaphore_signal(barrier, inc=1, device_id=device, device_id_type=MESH)
    pl.semaphore_wait(barrier, len(devices))


def others(axis):
    me, n = lax.axis_index(axis), lax.axis_size(axis)
    return [lax.rem(me + d, n) for d in range(1, n)]


def remote(src, dst, send, recv, device):
    return pltpu.make_async_remote_copy(
        src_ref=src, dst_ref=dst, send_sem=send, recv_sem=recv, device_id=device, device_id_type=MESH
    )


def swap_start(src_ref, dst_ref, axis, send, recv):
    me = lax.axis_index(axis)
    copies = []
    for d, peer in enumerate(others(axis)):
        copy = remote(src_ref.at[peer], dst_ref.at[me], send.at[d], recv.at[d], {axis: peer})
        copy.start()
        copies.append(copy)
    return copies


def upward_kernel(with_swap, *refs):
    if with_swap:
        x_ref, part_ref, out_ref, got_ref, zs, zr, xsend, xr, own, ts, tr = refs
    else:
        x_ref, out_ref, zs, zr, xsend, xr, own = refs
    me = lax.axis_index("seq")
    n = lax.axis_size("seq")
    high, low = me // 2, lax.rem(me, 2)
    line = n // 2
    partner = {"seq": high * 2 + 1 - low}
    devices = [{"seq": lax.rem(high + d, line) * 2 + low} for d in range(1, line)] + [partner]
    if with_swap:
        devices = devices + [{"tp": peer} for peer in others("tp")]
    greet(devices)
    mine = pltpu.make_async_copy(x_ref, out_ref.at[me], own)
    mine.start()

    def up(d):
        return remote(x_ref, out_ref.at[me], zs.at[d], zr.at[d], {"seq": (high + d) * 2 + low})

    def arrived(d):
        slot = out_ref.at[(high - d) * 2 + low]
        return remote(slot, slot, zs.at[d], zr.at[d], partner)

    def across(d):
        slot = out_ref.at[(high - d) * 2 + low]
        return remote(slot, slot, xsend.at[d], xr.at[d], partner)

    def across_own():
        return remote(x_ref, out_ref.at[me], xsend.at[0], xr.at[0], partner)

    across_own().start()
    for d in range(1, line):

        @pl.when(high + d < line)
        def _():
            up(d).start()

    if with_swap:
        swaps = swap_start(part_ref, got_ref, "tp", ts, tr)
    for d in range(1, line):

        @pl.when(high >= d)
        def _():
            arrived(d).wait_recv()
            across(d).start()

    across_own().wait()
    for d in range(1, line):

        @pl.when(high >= d)
        def _():
            across(d).wait()

        @pl.when(high + d < line)
        def _():
            up(d).wait_send()

    mine.wait()
    if with_swap:
        for copy in swaps:
            copy.wait()


def upward(x, part=None, cid=0):
    n = lax.axis_size("seq")
    line = max(n // 2, 1)
    scratch = [DMA((line,)), DMA((line,)), DMA((line,)), DMA((line,)), DMA]
    shapes = [jax.ShapeDtypeStruct((n,) + x.shape, x.dtype)]
    args = [x]
    if part is not None:
        scratch += [DMA((part.shape[0],)), DMA((part.shape[0],))]
        shapes.append(jax.ShapeDtypeStruct(part.shape, part.dtype))
        args.append(part)
    return pl.pallas_call(
        functools.partial(upward_kernel, part is not None),
        out_shape=shapes,
        in_specs=[VM] * len(args),
        out_specs=[VM] * len(shapes),
        scratch_shapes=scratch,
        compiler_params=pltpu.CompilerParams(collective_id=cid, has_side_effects=True),
    )(*args)


def rows_kernel(rows_ref, base_ref, out_ref, got, mine, ts, tr, gs, gr, own):
    me = lax.axis_index("tp")
    peers = others("tp")
    greet([{"tp": peer} for peer in peers])
    for copy in swap_start(rows_ref, got, "tp", ts, tr):
        copy.wait()
    total = rows_ref[me].astype(f32)
    for peer in peers:
        total = total + got[peer].astype(f32)
    quarter = rows_ref.shape[2]
    base = base_ref[:, pl.ds(pl.multiple_of(me * quarter, 128), quarter)]
    mine[...] = (base.astype(f32) + total).astype(bf16)
    copies = [
        remote(mine, out_ref.at[me], gs.at[d], gr.at[d], {"tp": peer})
        for d, peer in enumerate(peers)
    ]
    for copy in copies:
        copy.start()
    out_ref[me] = mine[...]
    for copy in copies:
        copy.wait()


def final_kernel(
    part_ref, stream_ref, place_ref, out_ref, got, send, mine, ts, tr, ss, sr, gs, gr
):
    me = lax.axis_index("tp")
    seq = lax.axis_index("seq")
    peers = others("tp")
    greet([{"tp": peer} for peer in peers] + [{"seq": peer} for peer in others("seq")])
    for copy in swap_start(part_ref, got, "tp", ts, tr):
        copy.wait()
    total = stream_ref[me].astype(f32) + part_ref[me].astype(f32)
    for peer in peers:
        total = total + got[peer].astype(f32)
    main = total.astype(bf16)
    ranks, cap, size = send.shape
    send[...] = t_mm(place_ref[...], main).astype(bf16).reshape(ranks, cap, size)
    copies = swap_start(send, mine, "seq", ss, sr)
    mine[seq] = send[seq]
    for copy in copies:
        copy.wait()
    cols = pl.ds(pl.multiple_of(me * size, 128), size)
    copies = [
        remote(mine, out_ref.at[:, :, cols], gs.at[d], gr.at[d], {"tp": peer})
        for d, peer in enumerate(peers)
    ]
    for copy in copies:
        copy.start()
    out_ref[:, :, cols] = mine[...]
    for copy in copies:
        copy.wait()


def on_device(
    byte_states, flags, stretch_owner, log_decay, w_x, w_z, w_bc, w_out, pad_vector, w_q, w_k, w_v, w_o
):
    rows, width = byte_states.shape
    heads = log_decay.shape[1]
    inner = w_x.shape[1]
    state_n = w_bc.shape[1] // 2
    ranks = lax.axis_size("seq")
    split = lax.axis_size("tp")
    count = stretch_owner.shape[0]
    quarter = width // split
    cap = max(2, 2 * count // ranks)
    wide = w_q.shape[0]
    shape = jax.ShapeDtypeStruct
    params = pltpu.CompilerParams(vmem_limit_bytes=48 * 1024 * 1024)

    def call(kernel, outs, *args):
        return pl.pallas_call(
            kernel,
            out_shape=outs,
            in_specs=[VM] * len(args),
            out_specs=[VM] * len(outs),
            compiler_params=params,
        )(*args)

    mixed, gate, cmat, grow, state = call(
        local_kernel,
        [
            shape((rows, inner), f32),
            shape((rows, inner), f32),
            shape((rows, state_n), bf16),
            shape((rows, heads), f32),
            shape((heads * state_n + 48, inner // heads), bf16),
        ],
        byte_states, w_x, w_z, w_bc, log_decay,
    )
    (every,) = upward(state, cid=1)
    part, partial_rows, base = call(
        functools.partial(encode_kernel, split),
        [
            shape((split, rows, quarter), bf16),
            shape((split, count, quarter), bf16),
            shape((count, width), bf16),
        ],
        every, mixed, gate, cmat, grow, w_out, flags.reshape(1, rows), byte_states,
    )
    peers = max(split - 1, 1)
    stretch_rows = pl.pallas_call(
        rows_kernel,
        out_shape=shape((split, count, quarter), bf16),
        in_specs=[VM] * 2,
        out_specs=VM,
        scratch_shapes=[
            pltpu.VMEM((split, count, quarter), bf16),
            pltpu.VMEM((count, quarter), bf16),
        ]
        + [DMA((peers,))] * 4
        + [DMA],
        compiler_params=pltpu.CompilerParams(collective_id=2, has_side_effects=True),
    )(partial_rows, base)
    queries, kv, stream, place = call(
        project_kernel,
        [
            shape((count, w_q.shape[1]), bf16),
            shape((count, 2 * w_k.shape[1]), bf16),
            shape((split, count, wide // split), bf16),
            shape((count, ranks * cap), bf16),
        ],
        stretch_rows, pad_vector.reshape(1, -1), w_q, w_k, w_v, stretch_owner,
    )
    every_kv, got = upward(kv, part, cid=3)
    group = math.gcd(ranks, 8)
    (partial_main,) = call(
        functools.partial(attend_kernel, group, split),
        [shape((split, count, wide // split), bf16)],
        queries, every_kv, w_o,
    )
    main_out = pl.pallas_call(
        final_kernel,
        out_shape=shape((ranks, cap, wide), bf16),
        in_specs=[VM] * 3,
        out_specs=VM,
        scratch_shapes=[
            pltpu.VMEM((split, count, wide // split), bf16),
            pltpu.VMEM((ranks, cap, wide // split), bf16),
            pltpu.VMEM((ranks, cap, wide // split), bf16),
        ]
        + [DMA((peers,))] * 2
        + [DMA((max(ranks - 1, 1),))] * 2
        + [DMA((peers,))] * 2,
        compiler_params=pltpu.CompilerParams(collective_id=4, has_side_effects=True),
    )(partial_main, stream, place)
    main_out = main_out.reshape(ranks * cap, wide)
    me = lax.axis_index("tp")
    own = lax.dynamic_index_in_dim(part, me, 0, keepdims=False).astype(f32)
    summed = own
    for d in range(1, split):
        peer = lax.rem(me + d, split)
        summed = summed + lax.dynamic_index_in_dim(got, peer, 0, keepdims=False).astype(f32)
    mine = lax.dynamic_slice_in_dim(byte_states, me * quarter, quarter, 1).astype(f32)
    return ((mine + summed).astype(bf16), main_out)


def solution(mesh):
    placed = (
        P("seq", None),
        P("seq"),
        P("seq", None),
        P("seq", "tp"),
        P(None, "tp"),
        P(None, "tp"),
        P(),
        P("tp", None),
        P(),
        P(None, "tp"),
        P(None, "tp"),
        P(None, "tp"),
        P("tp", None),
    )
    return jax.shard_map(
        on_device,
        mesh=mesh,
        in_specs=placed,
        out_specs=(P("seq", "tp"), P("seq", None)),
        check_vma=False,
    )
```

time: 321 us -> 138 us (0.43)
  waiting for transfers between devices: 143 us -> 0 us
  Pallas kernels: 0 us -> 109 us
  blocking collectives: 39.8 us -> 0 us
  matrix products: 33.9 us -> 0 us
  other arithmetic: 30.7 us -> 1.89 us
  local copies, waits for them, and re-layouts: 43 us -> 23.6 us
  between operations: 14.2 us -> 0.88 us
  starting transfers between devices: 13.2 us -> 0 us
    pallas_call x0 -> x8, Pallas kernels: none -> 109 us  [the longest x2 47.7 us: upward(): pl.pallas_call(functools.partial(upward_kernel, part is not None), out_sh...]
    psum x2 -> x0, waiting for transfers between devices: 66.7 us -> none  [the longest x1 34.9 us: on_device(): lax.psum(partial_enc.astype(jnp.bfloat16), 'tp').astype(jnp.float32)]
    all_gather x3 -> x0, waiting for transfers between devices: 64.7 us -> none  [the longest x1 42.5 us: on_device(): lax.all_gather(values_here, 'seq', axis=0, tiled=True)]
    all_gather x2 -> x0, blocking collectives: 39.8 us -> none  [the longest x1 21.2 us: carried_in(): lax.all_gather(part.astype(kind), axis)]
    dot_general x25 -> x0, matrix products: 32.2 us -> none  [the longest x4 6.27 us: attend_block(): jnp.einsum('hqk,khd->qhd', expo.astype(jnp.bfloat16), value_blk, preferre...]
    dynamic_update_slice x4 -> x0, local copies, waits for them, and re-layouts: 24.1 us -> none  [ssd_blocks(): final, outs = lax.scan(advance, start_state, blocks)]
    unnamed x44 -> x67, local copies, waits for them, and re-layouts: 3.06 us -> 23.6 us
    all_to_all x2 -> x0, starting transfers between devices: 12.8 us -> none  [the longest x1 7.29 us: on_device(): lax.all_to_all(send_pos.reshape(ranks, cap), 'seq', split_axis=0, concat_...]
  transfers between devices with their start and end apart: 7 -> 0, of which waited for: 6 -> 0; matrix products, arithmetic and copies ran while one was open for 14% -> 0% of each run, Pallas kernels for 0% -> 0%
where the time goes in v1:
time: 138 us; the launch traced here: 135 us
  Pallas kernels  109 us (79%)
  local copies, waits for them, and re-layouts  23.6 us (17%)
  other arithmetic  1.89 us (1%)
    pallas_call x2, Pallas kernels, upward(): pl.pallas_call(functools.partial(upward_kernel, part is not None), out_sh...  47.7 us
    pallas_call x1, Pallas kernels, on_device(): pl.pallas_call(final_kernel, out_shape=shape((ranks, cap, wide), bf16), i...  38.1 us
    unnamed x67, local copies, waits for them, and re-layouts  23.6 us
    pallas_call x4, Pallas kernels, call(): pl.pallas_call(kernel, out_shape=outs, in_specs=[VM] * len(args), out_spe...  11.8 us
    pallas_call x1, Pallas kernels, on_device(): pl.pallas_call(rows_kernel, out_shape=shape((split, count, quarter), bf16...  11.3 us

profile of v1, /device:TPU:0, one launch (start us, length us, event | category | flops | bytes accessed | tf_op | source)
XLA Modules:
  0.0 135.3 jit_solution(13387432905656793878)
XLA Ops:
  0.6 0.8 copy.15.decay_ref
  1.5 0.0 copy-start
  1.5 1.2 copy-done
  2.7 1.2 copy-done.10
  3.9 1.0 copy-done.16
  5.0 4.6 %shard_map.140 = (f32[512,512]{1,0:T(8,128)S(1)}, f32[512,512]{1,0:T(8,128)S(1)}, bf16[512,128]{1,0:T(8,128)(2,1)S(1)}, f32[512,4]{1,0:T(8,128)S(1)}, bf16[560,128]{1,0:T(8,128)(2,1)S(1)}) custom-call(bf16[512,1024]{1,0:T(8,128)(2,1)S(1)} %copy-done, bf16[1024,512]{1,0:T(8,128)(2,1)S(1)} %copy-done.10, bf16[1024,512]{1,0:T(8,128)(2,1)} %wz_ref.1, ...), custom_call_target="tpu_custom_call" | custom-call | tf_op jit(solution)/shard_map/pallas_call | solution.py:386
  9.5 0.0 copy-start.12
  9.5 1.0 copy-done.12
  10.5 1.0 copy-done.14
  11.5 0.7 copy-done.20
  12.2 0.7 copy-done.23
  12.9 16.6 %shard_map.141.every_ref = bf16[8,560,128]{2,1,0:T(8,128)(2,1)} custom-call(bf16[560,128]{1,0:T(8,128)(2,1)} %copy-done.23), custom_call_target="tpu_custom_call" | custom-call | tf_op jit(solution)/shard_map/pallas_call | solution.py:305
  29.5 0.0 copy-done.1
  29.5 0.0 copy-done.27
  29.5 0.0 copy-start.11
  29.5 1.2 copy-done.11
  30.7 1.2 copy-done.13
  32.0 1.2 copy-done.15
  33.2 0.9 copy-done.21
  34.1 4.4 %shard_map.142 = (bf16[4,512,256]{2,1,0:T(8,128)(2,1)S(1)}, bf16[4,128,256]{2,1,0:T(8,128)(2,1)S(1)}, bf16[128,1024]{1,0:T(8,128)(2,1)S(1)}) custom-call(bf16[8,560,128]{2,1,0:T(8,128)(2,1)} %shard_map.141.every_ref, f32[512,512]{1,0:T(8,128)S(1)} %copy-done.13, f32[512,512]{1,0:T(8,128)S(1)} %copy-done.15, bf16[512,128]{1,0:T(8,128)(2,1)S(1)} %get-tuple-element.19.c_ref, ...), custom_call_target="tpu_custom_call" | custom-call | tf_op jit(solution)/shard_map/pallas_call | solution.py:386
  38.6 0.0 copy-start.2
  38.6 1.0 copy-done.2
  39.6 0.7 copy-done.18
  40.3 0.7 copy-done.19
  41.0 11.3 %shard_map.143.rows_ref = bf16[4,128,256]{2,1,0:T(8,128)(2,1)} custom-call(bf16[4,128,256]{2,1,0:T(8,128)(2,1)} %copy-done.18, bf16[128,1024]{1,0:T(8,128)(2,1)} %copy-done.19), custom_call_target="tpu_custom_call" | custom-call | tf_op jit(solution)/shard_map/pallas_call | solution.py:416
  52.3 0.0 copy-done.31
  52.3 0.1 copy.16.owner_ref
  52.4 0.0 copy-done.30
  52.4 0.0 copy-done.5
  52.4 0.0 copy-done.6
  52.4 0.0 copy-start.7
  52.4 1.3 copy-done.7
  53.7 0.9 copy-done.9
  54.7 1.1 shard_map.144
  55.8 0.0 copy-start.17
  55.8 0.7 copy-done.17
  56.5 0.7 copy-done.22
  57.2 0.6 copy-done.24
  57.8 0.6 copy-done.26
  58.4 31.1 %shard_map.145 = (bf16[8,128,768]{2,1,0:T(8,128)(2,1)}, bf16[4,512,256]{2,1,0:T(8,128)(2,1)}) custom-call(bf16[128,768]{1,0:T(8,128)(2,1)} %copy-done.22, bf16[4,512,256]{2,1,0:T(8,128)(2,1)} %copy-done.2), custom_call_target="tpu_custom_call" | custom-call | tf_op jit(solution)/shard_map/pallas_call | solution.py:305
  89.6 1.4 %copy-done.3 = bf16[8,128,768]{2,1,0:T(8,128)(2,1)S(1)} copy-done((bf16[8,128,768]{2,1,0:T(8,128)(2,1)S(1)}, bf16[8,128,768]{2,1,0:T(8,128)(2,1)}, u32[]{:S(2)}) %copy-start.3) | copy-done | bytes 1572888
  91.0 0.9 copy-done.25
  91.8 1.7 %shard_map.146.part_ref = bf16[4,128,384]{2,1,0:T(8,128)(2,1)S(1)} custom-call(bf16[128,384]{1,0:T(8,128)(2,1)S(1)} %copy-done.25, bf16[8,128,768]{2,1,0:T(8,128)(2,1)S(1)} %copy-done.3, bf16[384,1536]{1,0:T(8,128)(2,1)S(1)} %copy-done.8), custom_call_target="tpu_custom_call" | custom-call | tf_op jit(solution)/shard_map/pallas_call | solution.py:386
  93.6 0.0 copy-start.4
  93.6 0.7 copy-done.4
  94.3 38.1 %shard_map.147 = bf16[8,32,1536]{2,1,0:T(8,128)(2,1)} custom-call(bf16[4,128,384]{2,1,0:T(8,128)(2,1)} %copy-done.4, bf16[4,128,384]{2,1,0:T(8,128)(2,1)} %copy-done.17, bf16[128,256]{1,0:T(8,128)(2,1)} %copy-done.26), custom_call_target="tpu_custom_call" | custom-call | tf_op jit(solution)/shard_map/pallas_call | solution.py:446
  132.5 1.9 %fusion = bf16[512,256]{1,0:T(8,128)(2,1)} fusion(bf16[4,512,256]{2,1,0:T(8,128)(2,1)S(1)} %copy-done.29, s32[]{:T(128)S(6)} %select_n.20, s32[]{:T(128)S(6)} %select_n.19, s32[]{:T(128)S(6)} %select_n.18, bf16[4,512,256]{2,1,0:T(8,128)(2,1)} %copy-done.2, s32[]{:T(128)S(6)} %select_n.17, bf16[512,1024]{1,0:T(8,128)(2,1)S(1)} %copy-done.1, s32[]{:T(128)S(6)} %select_n.16), kind=kLoop, calls=%fused_computation.1 | loop fusion | flops 1310720 | bytes 1572884 | tf_op jit(solution)/shard_map/convert_element_type | solution.py:469
  134.4 0.9 copy.18
  (29 shorter events, 0.1 us)
Async XLA Ops:
  1.5 1.2 copy-start
  2.7 1.2 copy-start.10
  3.9 1.0 copy-start.16
  9.5 1.0 copy-start.12
  10.5 1.0 copy-start.14
  11.5 0.7 copy-start.20
  12.2 0.7 copy-start.23
  12.9 16.6 %copy-start.1 = (bf16[512,1024]{1,0:T(8,128)(2,1)S(1)}, bf16[512,1024]{1,0:T(8,128)(2,1)}, u32[]{:S(2)}) copy-start(bf16[512,1024]{1,0:T(8,128)(2,1)} %bytes_ref.3) | copy-start | bytes 3145732
  12.9 16.6 %copy-start.27 = (s32[512]{0:T(512)S(1)}, s32[512]{0:T(512)}, u32[]{:S(2)}) copy-start(s32[512]{0:T(512)} %param.14) | copy-start | bytes 6148
  29.5 1.2 copy-start.11
  30.7 1.2 copy-start.13
  31.9 1.2 copy-start.15
  33.2 0.9 copy-start.21
  34.1 18.1 %copy-start.31 = (s32[128,1]{0,1:T(1,128)S(1)}, s32[128,1]{0,1:T(1,128)}, u32[]{:S(2)}) copy-start(s32[128,1]{0,1:T(1,128)} %param.15) | copy-start | bytes 1540
  34.1 18.3 %copy-start.30 = (bf16[512]{0:T(512)(128)(2,1)S(1)}, bf16[512]{0:T(512)(128)(2,1)}, u32[]{:S(2)}) copy-start(bf16[512]{0:T(512)(128)(2,1)} %param.21) | copy-start | bytes 3076
  34.1 18.3 %copy-start.5 = (bf16[1536,384]{1,0:T(8,128)(2,1)S(1)}, bf16[1536,384]{1,0:T(8,128)(2,1)}, u32[]{:S(2)}) copy-start(bf16[1536,384]{1,0:T(8,128)(2,1)} %wq_ref.1) | copy-start | bytes 3538948
  34.1 18.3 %copy-start.6 = (bf16[1536,384]{1,0:T(8,128)(2,1)S(1)}, bf16[1536,384]{1,0:T(8,128)(2,1)}, u32[]{:S(2)}) copy-start(bf16[1536,384]{1,0:T(8,128)(2,1)} %wk_ref.1) | copy-start | bytes 3538948
  38.6 1.0 copy-start.2
  39.6 0.7 copy-start.18
  40.3 0.7 copy-start.19
  52.4 1.3 copy-start.7
  53.7 0.9 copy-start.9
  55.8 0.8 copy-start.17
  56.5 0.7 copy-start.22
  57.2 0.6 copy-start.24
  57.8 0.6 copy-start.26
  58.4 31.1 %copy-start.8 = (bf16[384,1536]{1,0:T(8,128)(2,1)S(1)}, bf16[384,1536]{1,0:T(8,128)(2,1)}, u32[]{:S(2)}) copy-start(bf16[384,1536]{1,0:T(8,128)(2,1)} %wo_ref.1) | copy-start | bytes 3538948
  89.5 1.4 %copy-start.3 = (bf16[8,128,768]{2,1,0:T(8,128)(2,1)S(1)}, bf16[8,128,768]{2,1,0:T(8,128)(2,1)}, u32[]{:S(2)}) copy-start(bf16[8,128,768]{2,1,0:T(8,128)(2,1)} %get-tuple-element.27.all_ref) | copy-start | bytes 4718596
  91.0 0.9 copy-start.25
  93.6 0.7 copy-start.4
  94.3 38.2 %copy-start.29 = (bf16[4,512,256]{2,1,0:T(8,128)(2,1)S(1)}, bf16[4,512,256]{2,1,0:T(8,128)(2,1)}, u32[]{:S(2)}) copy-start(bf16[4,512,256]{2,1,0:T(8,128)(2,1)} %get-tuple-element.25) | copy-start | bytes 3145732
  132.5 1.9 %copy-start.28 = (bf16[8,32,1536]{2,1,0:T(8,128)(2,1)S(1)}, bf16[8,32,1536]{2,1,0:T(8,128)(2,1)}, u32[]{:S(2)}) copy-start(bf16[8,32,1536]{2,1,0:T(8,128)(2,1)} %shard_map.147) | copy-start | bytes 2359300

commit v2 on v1

--- a/solution.py
+++ b/solution.py
@@ -15,6 +15,7 @@
 MESH = pl.DeviceIdType.MESH
 VM = pl.BlockSpec(memory_space=pltpu.VMEM)
 DMA = pltpu.SemaphoreType.DMA
+LIMIT = 8 * 1024 * 1024
 
 
 def mm(a, b):
@@ -230,61 +231,73 @@
 
 def upward_kernel(with_swap, *refs):
     if with_swap:
-        x_ref, part_ref, out_ref, got_ref, zs, zr, xsend, xr, own, ts, tr = refs
+        x_ref, part_ref, out_ref, got_ref, zs, zr, ws, wr, own, ts, tr = refs
     else:
-        x_ref, out_ref, zs, zr, xsend, xr, own = refs
+        x_ref, out_ref, zs, zr, ws, wr, own = refs
     me = lax.axis_index("seq")
     n = lax.axis_size("seq")
     high, low = me // 2, lax.rem(me, 2)
     line = n // 2
+    pieces = zs.shape[1]
+    size = x_ref.shape[0] // pieces
     partner = {"seq": high * 2 + 1 - low}
-    devices = [{"seq": lax.rem(high + d, line) * 2 + low} for d in range(1, line)] + [partner]
+    steps = sorted({1, line - 1} - {0}) if line > 1 else []
+    devices = [{"seq": lax.rem(high + d, line) * 2 + low} for d in steps] + [partner]
     if with_swap:
         devices = devices + [{"tp": peer} for peer in others("tp")]
     greet(devices)
     mine = pltpu.make_async_copy(x_ref, out_ref.at[me], own)
     mine.start()
 
-    def up(d):
-        return remote(x_ref, out_ref.at[me], zs.at[d], zr.at[d], {"seq": (high + d) * 2 + low})
-
-    def arrived(d):
-        slot = out_ref.at[(high - d) * 2 + low]
-        return remote(slot, slot, zs.at[d], zr.at[d], partner)
-
-    def across(d):
-        slot = out_ref.at[(high - d) * 2 + low]
-        return remote(slot, slot, xsend.at[d], xr.at[d], partner)
-
-    def across_own():
-        return remote(x_ref, out_ref.at[me], xsend.at[0], xr.at[0], partner)
-
-    across_own().start()
-    for d in range(1, line):
-
-        @pl.when(high + d < line)
-        def _():
-            up(d).start()
-
+    def source(d, c):
+        rows = pl.ds(c * size, size)
+        return x_ref.at[rows] if d == 0 else out_ref.at[(high - d) * 2 + low, rows]
+
+    def slot(d, c):
+        return out_ref.at[(high - d) * 2 + low, pl.ds(c * size, size)]
+
+    def up(d, c):
+        device = {"seq": (high + 1) * 2 + low}
+        return remote(source(d, c), slot(d, c), zs.at[d, c], zr.at[d + 1, c], device)
+
+    def arrived(d, c):
+        return remote(slot(d, c), slot(d, c), zs.at[d, c], zr.at[d, c], partner)
+
+    def across(d, c):
+        return remote(source(d, c), slot(d, c), ws.at[d, c], wr.at[d, c], partner)
+
+    def send_on(d, c):
+        if d < line - 1:
+
+            @pl.when(high + 1 < line)
+            def _():
+                up(d, c).start()
+
+        across(d, c).start()
+
+    for c in range(pieces):
+        send_on(0, c)
     if with_swap:
         swaps = swap_start(part_ref, got_ref, "tp", ts, tr)
     for d in range(1, line):
 
         @pl.when(high >= d)
         def _():
-            arrived(d).wait_recv()
-            across(d).start()
-
-    across_own().wait()
-    for d in range(1, line):
+            for c in range(pieces):
+                arrived(d, c).wait_recv()
+                send_on(d, c)
+
+    for d in range(line):
 
         @pl.when(high >= d)
         def _():
-            across(d).wait()
-
-        @pl.when(high + d < line)
-        def _():
-            up(d).wait_send()
+            for c in range(pieces):
+                across(d, c).wait()
+                if d < line - 1:
+
+                    @pl.when(high + 1 < line)
+                    def _():
+                        up(d, c).wait_send()
 
     mine.wait()
     if with_swap:
@@ -295,7 +308,9 @@
 def upward(x, part=None, cid=0):
     n = lax.axis_size("seq")
     line = max(n // 2, 1)
-    scratch = [DMA((line,)), DMA((line,)), DMA((line,)), DMA((line,)), DMA]
+    fits = [c for c in (4, 5, 2, 1) if x.shape[0] % (16 * c) == 0 and c * line <= 32]
+    pieces = fits[0]
+    scratch = [DMA((line + 1, pieces))] * 4 + [DMA]
     shapes = [jax.ShapeDtypeStruct((n,) + x.shape, x.dtype)]
     args = [x]
     if part is not None:
@@ -308,7 +323,9 @@
         in_specs=[VM] * len(args),
         out_specs=[VM] * len(shapes),
         scratch_shapes=scratch,
-        compiler_params=pltpu.CompilerParams(collective_id=cid, has_side_effects=True),
+        compiler_params=pltpu.CompilerParams(
+            collective_id=cid, has_side_effects=True, vmem_limit_bytes=LIMIT
+        ),
     )(*args)
 
 
@@ -336,11 +353,14 @@
 
 
 def final_kernel(
-    part_ref, stream_ref, place_ref, out_ref, got, send, mine, ts, tr, ss, sr, gs, gr
+    part_ref, stream_ref, place_ref, out_ref, got, send, mine, ts, tr, ss, sr, cs, cr, ps, pr
 ):
     me = lax.axis_index("tp")
     seq = lax.axis_index("seq")
     peers = others("tp")
+    groups = lax.axis_size("tp") // 2
+    high, low = me // 2, lax.rem(me, 2)
+    ranks, cap, size = send.shape
     greet([{"tp": peer} for peer in peers] + [{"seq": peer} for peer in others("seq")])
     for copy in swap_start(part_ref, got, "tp", ts, tr):
         copy.wait()
@@ -348,22 +368,43 @@
     for peer in peers:
         total = total + got[peer].astype(f32)
     main = total.astype(bf16)
-    ranks, cap, size = send.shape
     send[...] = t_mm(place_ref[...], main).astype(bf16).reshape(ranks, cap, size)
     copies = swap_start(send, mine, "seq", ss, sr)
     mine[seq] = send[seq]
-    for copy in copies:
-        copy.wait()
-    cols = pl.ds(pl.multiple_of(me * size, 128), size)
-    copies = [
-        remote(mine, out_ref.at[:, :, cols], gs.at[d], gr.at[d], {"tp": peer})
-        for d, peer in enumerate(peers)
-    ]
-    for copy in copies:
-        copy.start()
-    out_ref[:, :, cols] = mine[...]
-    for copy in copies:
-        copy.wait()
+
+    def spot(e, d):
+        column = (lax.rem(high - e + groups, groups) * 2 + low) * size
+        return out_ref.at[lax.rem(seq - d + ranks, ranks), :, pl.ds(pl.multiple_of(column, 128), size)]
+
+    def held(e, d):
+        return mine.at[lax.rem(seq - d + ranks, ranks)] if e == 0 else spot(e, d)
+
+    def direct(e, d):
+        device = {"tp": lax.rem(high + e, groups) * 2 + low}
+        return remote(held(0, d), spot(0, d), cs.at[e, d], cr.at[e, d], device)
+
+    def pair(e, d):
+        device = {"tp": high * 2 + 1 - low}
+        return remote(held(e, d), spot(e, d), ps.at[e, d], pr.at[e, d], device)
+
+    for d in range(ranks):
+        if d > 0:
+            copies[d - 1].wait_recv()
+        for e in range(1, groups):
+            direct(e, d).start()
+        pair(0, d).start()
+    for d in range(ranks):
+        for e in range(1, groups):
+            direct(e, d).wait_recv()
+            pair(e, d).start()
+    out_ref[:, :, pl.ds(pl.multiple_of(me * size, 128), size)] = mine[...]
+    for d in range(ranks):
+        if d > 0:
+            copies[d - 1].wait_send()
+        for e in range(groups):
+            if e > 0:
+                direct(e, d).wait_send()
+            pair(e, d).wait()
 
 
 def on_device(
@@ -380,7 +421,7 @@
     cap = max(2, 2 * count // ranks)
     wide = w_q.shape[0]
     shape = jax.ShapeDtypeStruct
-    params = pltpu.CompilerParams(vmem_limit_bytes=48 * 1024 * 1024)
+    params = pltpu.CompilerParams(vmem_limit_bytes=3 * LIMIT)
 
     def call(kernel, outs, *args):
         return pl.pallas_call(
@@ -424,7 +465,9 @@
         ]
         + [DMA((peers,))] * 4
         + [DMA],
-        compiler_params=pltpu.CompilerParams(collective_id=2, has_side_effects=True),
+        compiler_params=pltpu.CompilerParams(
+            collective_id=2, has_side_effects=True, vmem_limit_bytes=LIMIT
+        ),
     )(partial_rows, base)
     queries, kv, stream, place = call(
         project_kernel,
@@ -455,8 +498,10 @@
         ]
         + [DMA((peers,))] * 2
         + [DMA((max(ranks - 1, 1),))] * 2
-        + [DMA((peers,))] * 2,
-        compiler_params=pltpu.CompilerParams(collective_id=4, has_side_effects=True),
+        + [DMA((split // 2, ranks))] * 4,
+        compiler_params=pltpu.CompilerParams(
+            collective_id=4, has_side_effects=True, vmem_limit_bytes=LIMIT
+        ),
     )(partial_main, stream, place)
     main_out = main_out.reshape(ranks * cap, wide)
     me = lax.axis_index("tp")

time: 138 us -> 90.6 us (0.66); the launches traced: 135 us -> 90.2 us
  Pallas kernels: 109 us -> 78.4 us
  local copies, waits for them, and re-layouts: 23.6 us -> 9.12 us
    unnamed x67 -> x27, local copies, waits for them, and re-layouts: 23.6 us -> 9.11 us
    pallas_call x1, Pallas kernels: 38.1 us -> 24.4 us  [on_device(): pl.pallas_call(final_kernel, out_shape=shape((ranks, cap, wide), bf16), i...]
    pallas_call x2, Pallas kernels: 47.7 us -> 35.2 us  [upward(): pl.pallas_call(functools.partial(upward_kernel, part is not None), out_sh...]
    pallas_call x4, Pallas kernels: 11.8 us -> 9.21 us  [call(): pl.pallas_call(kernel, out_shape=outs, in_specs=[VM] * len(args), out_spe...]
    pallas_call x1, Pallas kernels: 11.3 us -> 9.64 us  [on_device(): pl.pallas_call(rows_kernel, out_shape=shape((split, count, quarter), bf16...]
where the time goes in v2:
time: 90.6 us; the launch traced here: 90.2 us
  Pallas kernels  78.4 us (87%)
  local copies, waits for them, and re-layouts  9.12 us (10%)
  other arithmetic  1.83 us (2%)
    pallas_call x2, Pallas kernels, upward(): pl.pallas_call(functools.partial(upward_kernel, part is not None), out_sh...  35.2 us
    pallas_call x1, Pallas kernels, on_device(): pl.pallas_call(final_kernel, out_shape=shape((ranks, cap, wide), bf16), i...  24.4 us
    pallas_call x1, Pallas kernels, on_device(): pl.pallas_call(rows_kernel, out_shape=shape((split, count, quarter), bf16...  9.64 us
    pallas_call x4, Pallas kernels, call(): pl.pallas_call(kernel, out_shape=outs, in_specs=[VM] * len(args), out_spe...  9.21 us
    unnamed x27, local copies, waits for them, and re-layouts  9.11 us
    convert_element_type x1, other arithmetic, on_device(): return ((mine + summed).astype(bf16), main_out)  1.83 us

profile of v2, /device:TPU:0, one launch (start us, length us, event | category | flops | bytes accessed | tf_op | source)
XLA Modules:
  0.0 90.2 jit_solution(15812156409863654735)
XLA Ops:
  0.6 0.8 copy.15.decay_ref
  1.5 0.0 copy-start
  1.5 1.2 %copy-done = bf16[512,1024]{1,0:T(8,128)(2,1)S(1)} copy-done((bf16[512,1024]{1,0:T(8,128)(2,1)S(1)}, bf16[512,1024]{1,0:T(8,128)(2,1)}, u32[]{:S(2)}) %copy-start) | copy-done | bytes 1048600
  2.7 0.0 copy-start.5
  2.7 1.2 %copy-done.5 = bf16[1024,512]{1,0:T(8,128)(2,1)S(1)} copy-done((bf16[1024,512]{1,0:T(8,128)(2,1)S(1)}, bf16[1024,512]{1,0:T(8,128)(2,1)}, u32[]{:S(2)}) %copy-start.5) | copy-done | bytes 1048600
  3.9 0.0 copy-start.6
  3.9 1.2 %copy-done.6 = bf16[1024,512]{1,0:T(8,128)(2,1)S(1)} copy-done((bf16[1024,512]{1,0:T(8,128)(2,1)S(1)}, bf16[1024,512]{1,0:T(8,128)(2,1)}, u32[]{:S(2)}) %copy-start.6) | copy-done | bytes 1048600
  5.2 0.0 copy-start.8
  5.2 1.0 %copy-done.8 = bf16[1024,256]{1,0:T(8,128)(2,1)S(1)} copy-done((bf16[1024,256]{1,0:T(8,128)(2,1)S(1)}, bf16[1024,256]{1,0:T(8,128)(2,1)}, u32[]{:S(2)}) %copy-start.8) | copy-done | bytes 524312
  6.2 3.3 %shard_map.140 = (f32[512,512]{1,0:T(8,128)S(1)}, f32[512,512]{1,0:T(8,128)S(1)}, bf16[512,128]{1,0:T(8,128)(2,1)S(1)}, f32[512,4]{1,0:T(8,128)S(1)}, bf16[560,128]{1,0:T(8,128)(2,1)S(1)}) custom-call(bf16[512,1024]{1,0:T(8,128)(2,1)S(1)} %copy-done, bf16[1024,512]{1,0:T(8,128)(2,1)S(1)} %copy-done.5, bf16[1024,512]{1,0:T(8,128)(2,1)S(1)} %copy-done.6, ...), custom_call_target="tpu_custom_call" | custom-call | tf_op jit(solution)/shard_map/pallas_call | solution.py:427
  9.5 0.0 copy-start.7
  9.6 0.0 copy-start.9
  9.6 11.1 %shard_map.141.every_ref = bf16[8,560,128]{2,1,0:T(8,128)(2,1)S(1)} custom-call(bf16[560,128]{1,0:T(8,128)(2,1)S(1)} %get-tuple-element.16.refs_0_), custom_call_target="tpu_custom_call" | custom-call | tf_op jit(solution)/shard_map/pallas_call | solution.py:320
  20.7 0.0 copy-done.7
  20.7 0.0 copy-done.9
  20.7 0.0 copy-start.11
  20.8 0.0 copy-start.10
  20.8 0.0 copy-start.1
  20.8 3.0 %shard_map.142 = (bf16[4,512,256]{2,1,0:T(8,128)(2,1)S(1)}, bf16[4,128,256]{2,1,0:T(8,128)(2,1)S(1)}, bf16[128,1024]{1,0:T(8,128)(2,1)S(1)}) custom-call(bf16[8,560,128]{2,1,0:T(8,128)(2,1)S(1)} %shard_map.141.every_ref, f32[512,512]{1,0:T(8,128)S(1)} %get-tuple-element.17.mixed_ref, f32[512,512]{1,0:T(8,128)S(1)} %get-tuple-element.18.gate_ref, ...), custom_call_target="tpu_custom_call" | custom-call | tf_op jit(solution)/shard_map/pallas_call | solution.py:427
  23.8 9.6 %shard_map.143.rows_ref = bf16[4,128,256]{2,1,0:T(8,128)(2,1)S(1)} custom-call(bf16[4,128,256]{2,1,0:T(8,128)(2,1)S(1)} %get-tuple-element.22.rows_ref, bf16[128,1024]{1,0:T(8,128)(2,1)S(1)} %get-tuple-element.23.base_ref), custom_call_target="tpu_custom_call" | custom-call | tf_op jit(solution)/shard_map/pallas_call | solution.py:457
  33.5 0.0 copy-done.11
  33.5 0.1 copy.16.owner_ref
  33.6 0.0 copy-done.10
  33.6 0.0 copy-done.1
  33.6 0.0 copy-start.2
  33.6 1.3 %copy-done.2 = bf16[1536,384]{1,0:T(8,128)(2,1)S(1)} copy-done((bf16[1536,384]{1,0:T(8,128)(2,1)S(1)}, bf16[1536,384]{1,0:T(8,128)(2,1)}, u32[]{:S(2)}) %copy-start.2) | copy-done | bytes 1179672
  34.9 0.0 copy-start.3
  34.9 1.3 %copy-done.3 = bf16[1536,384]{1,0:T(8,128)(2,1)S(1)} copy-done((bf16[1536,384]{1,0:T(8,128)(2,1)S(1)}, bf16[1536,384]{1,0:T(8,128)(2,1)}, u32[]{:S(2)}) %copy-start.3) | copy-done | bytes 1179672
  36.2 1.1 %shard_map.144 = (bf16[128,384]{1,0:T(8,128)(2,1)S(1)}, bf16[128,768]{1,0:T(8,128)(2,1)S(1)}, bf16[4,128,384]{2,1,0:T(8,128)(2,1)S(1)}, bf16[128,256]{1,0:T(8,128)(2,1)S(1)}) custom-call(bf16[4,128,256]{2,1,0:T(8,128)(2,1)S(1)} %shard_map.143.rows_ref, bf16[1,512]{1,0:T(2,128)(2,1)S(1)} %reshape.21.pad_ref, bf16[1536,384]{1,0:T(8,128)(2,1)S(1)} %copy-done.1, ...), custom_call_target="tpu_custom_call" | custom-call | tf_op jit(solution)/shard_map/pallas_call | solution.py:427
  37.3 0.0 copy-start.4
  37.3 24.0 %shard_map.145 = (bf16[8,128,768]{2,1,0:T(8,128)(2,1)S(1)}, bf16[4,512,256]{2,1,0:T(8,128)(2,1)S(1)}) custom-call(bf16[128,768]{1,0:T(8,128)(2,1)S(1)} %get-tuple-element.24.refs_0_, bf16[4,512,256]{2,1,0:T(8,128)(2,1)S(1)} %get-tuple-element.21.refs_1_), custom_call_target="tpu_custom_call" | custom-call | tf_op jit(solution)/shard_map/pallas_call | solution.py:320
  61.3 0.0 copy-done.4
  61.3 1.7 %shard_map.146.part_ref = bf16[4,128,384]{2,1,0:T(8,128)(2,1)S(1)} custom-call(bf16[128,384]{1,0:T(8,128)(2,1)S(1)} %get-tuple-element.26.q_ref, bf16[8,128,768]{2,1,0:T(8,128)(2,1)S(1)} %get-tuple-element.27.all_ref, bf16[384,1536]{1,0:T(8,128)(2,1)S(1)} %copy-done.4), custom_call_target="tpu_custom_call" | custom-call | tf_op jit(solution)/shard_map/pallas_call | solution.py:427
  63.1 24.4 %shard_map.147 = bf16[8,32,1536]{2,1,0:T(8,128)(2,1)S(1)} custom-call(bf16[4,128,384]{2,1,0:T(8,128)(2,1)S(1)} %shard_map.146.part_ref, bf16[4,128,384]{2,1,0:T(8,128)(2,1)S(1)} %get-tuple-element.28.stream_ref, bf16[128,256]{1,0:T(8,128)(2,1)S(1)} %get-tuple-element.29.place_ref), custom_call_target="tpu_custom_call" | custom-call | tf_op jit(solution)/shard_map/pallas_call | solution.py:489
  87.5 1.8 %fusion = bf16[512,256]{1,0:T(8,128)(2,1)} fusion(bf16[4,512,256]{2,1,0:T(8,128)(2,1)S(1)} %get-tuple-element.25, s32[]{:T(128)S(6)} %select_n.20, s32[]{:T(128)S(6)} %select_n.19, s32[]{:T(128)S(6)} %select_n.18, bf16[4,512,256]{2,1,0:T(8,128)(2,1)S(1)} %get-tuple-element.21.refs_1_, s32[]{:T(128)S(6)} %select_n.17, bf16[512,1024]{1,0:T(8,128)(2,1)} %bytes_ref.3, ...), kind=kLoop, calls=%fused_computation.1 | loop fusion | flops 1310720 | bytes 1572884 | tf_op jit(solution)/shard_map/convert_element_type | solution.py:514
  89.3 0.9 copy.18
  (1 shorter events, 0.0 us)
Async XLA Ops:
  1.5 1.2 %copy-start = (bf16[512,1024]{1,0:T(8,128)(2,1)S(1)}, bf16[512,1024]{1,0:T(8,128)(2,1)}, u32[]{:S(2)}) copy-start(bf16[512,1024]{1,0:T(8,128)(2,1)} %bytes_ref.3) | copy-start | bytes 3145732
  2.7 1.2 %copy-start.5 = (bf16[1024,512]{1,0:T(8,128)(2,1)S(1)}, bf16[1024,512]{1,0:T(8,128)(2,1)}, u32[]{:S(2)}) copy-start(bf16[1024,512]{1,0:T(8,128)(2,1)} %wx_ref.1) | copy-start | bytes 3145732
  3.9 1.2 %copy-start.6 = (bf16[1024,512]{1,0:T(8,128)(2,1)S(1)}, bf16[1024,512]{1,0:T(8,128)(2,1)}, u32[]{:S(2)}) copy-start(bf16[1024,512]{1,0:T(8,128)(2,1)} %wz_ref.1) | copy-start | bytes 3145732
  5.2 1.0 %copy-start.8 = (bf16[1024,256]{1,0:T(8,128)(2,1)S(1)}, bf16[1024,256]{1,0:T(8,128)(2,1)}, u32[]{:S(2)}) copy-start(bf16[1024,256]{1,0:T(8,128)(2,1)} %wbc_ref.1) | copy-start | bytes 1572868
  9.5 11.2 %copy-start.7 = (bf16[512,1024]{1,0:T(8,128)(2,1)S(1)}, bf16[512,1024]{1,0:T(8,128)(2,1)}, u32[]{:S(2)}) copy-start(bf16[512,1024]{1,0:T(8,128)(2,1)} %wout_ref.1) | copy-start | bytes 3145732
  9.6 11.2 %copy-start.9 = (s32[512]{0:T(512)S(1)}, s32[512]{0:T(512)}, u32[]{:S(2)}) copy-start(s32[512]{0:T(512)} %param.14) | copy-start | bytes 6148
  20.7 12.7 %copy-start.11 = (s32[128,1]{0,1:T(1,128)S(1)}, s32[128,1]{0,1:T(1,128)}, u32[]{:S(2)}) copy-start(s32[128,1]{0,1:T(1,128)} %param.15) | copy-start | bytes 1540
  20.8 12.8 %copy-start.10 = (bf16[512]{0:T(512)(128)(2,1)S(1)}, bf16[512]{0:T(512)(128)(2,1)}, u32[]{:S(2)}) copy-start(bf16[512]{0:T(512)(128)(2,1)} %param.21) | copy-start | bytes 3076
  20.8 12.8 %copy-start.1 = (bf16[1536,384]{1,0:T(8,128)(2,1)S(1)}, bf16[1536,384]{1,0:T(8,128)(2,1)}, u32[]{:S(2)}) copy-start(bf16[1536,384]{1,0:T(8,128)(2,1)} %wq_ref.1) | copy-start | bytes 3538948
  33.6 1.3 %copy-start.2 = (bf16[1536,384]{1,0:T(8,128)(2,1)S(1)}, bf16[1536,384]{1,0:T(8,128)(2,1)}, u32[]{:S(2)}) copy-start(bf16[1536,384]{1,0:T(8,128)(2,1)} %wk_ref.1) | copy-start | bytes 3538948
  34.9 1.3 %copy-start.3 = (bf16[1536,384]{1,0:T(8,128)(2,1)S(1)}, bf16[1536,384]{1,0:T(8,128)(2,1)}, u32[]{:S(2)}) copy-start(bf16[1536,384]{1,0:T(8,128)(2,1)} %wv_ref.1) | copy-start | bytes 3538948
  37.3 24.0 %copy-start.4 = (bf16[384,1536]{1,0:T(8,128)(2,1)S(1)}, bf16[384,1536]{1,0:T(8,128)(2,1)}, u32[]{:S(2)}) copy-start(bf16[384,1536]{1,0:T(8,128)(2,1)} %wo_ref.1) | copy-start | bytes 3538948

commit v3 on v2

--- a/solution.py
+++ b/solution.py
@@ -14,8 +14,13 @@
 bf16 = jnp.bfloat16
 MESH = pl.DeviceIdType.MESH
 VM = pl.BlockSpec(memory_space=pltpu.VMEM)
+HBM = pl.BlockSpec(memory_space=pltpu.HBM)
 DMA = pltpu.SemaphoreType.DMA
 LIMIT = 8 * 1024 * 1024
+
+
+def cost(us):
+    return pl.CostEstimate(flops=us * 10**9, bytes_accessed=us * 3 * 10**6, transcendentals=0)
 
 
 def mm(a, b):
@@ -43,25 +48,44 @@
 
 
 def local_kernel(
-    bytes_ref, wx_ref, wz_ref, wbc_ref, decay_ref, mixed_ref, gate_ref, c_ref, grow_ref, state_ref
+    bytes_hbm, wx_hbm, wz_hbm, wbc_hbm, decay_ref, mixed_ref, gate_ref, c_ref, grow_ref, state_ref,
+    bytes_ref, wx_ref, wz_ref, wbc_ref, sems,
 ):
+    fetches = []
+    for i, (src, dst) in enumerate(
+        ((bytes_hbm, bytes_ref), (wbc_hbm, wbc_ref), (wx_hbm, wx_ref), (wz_hbm, wz_ref))
+    ):
+        half = src.shape[0] // 2
+        for j in range(2):
+            span = pl.ds(j * half, half)
+            copy = pltpu.make_async_copy(src.at[span], dst.at[span], sems.at[i, j])
+            copy.start()
+            fetches.append(copy)
+
+    def ready(i):
+        fetches[2 * i].wait()
+        fetches[2 * i + 1].wait()
+
     rows = bytes_ref.shape[0]
-    heads = decay_ref.shape[1]
+    heads = decay_ref.shape[0]
     state_n = wbc_ref.shape[1] // 2
     p = wx_ref.shape[1] // heads
-    wide = bytes_ref[...].astype(f32)
-    normed = (wide * lax.rsqrt(jnp.mean(wide * wide, axis=-1, keepdims=True) + eps)).astype(bf16)
-    bc = mm(normed, wbc_ref[...]).astype(bf16)
-    bmat, cmat = bc[:, :state_n], bc[:, state_n:]
-    c_ref[...] = cmat
-    xs = mm(normed, wx_ref[...]).astype(bf16)
     parts = three(decay_ref[...])
     lower = (iota((rows, rows), 0) >= iota((rows, rows), 1)).astype(f32).astype(bf16)
     upper = (iota((rows, rows), 0) <= iota((rows, rows), 1)).astype(f32).astype(bf16)
     ones = jnp.ones((rows, state_n), bf16)
-    cum = sum(mm(lower, part) for part in parts)
-    cum_row = sum(t_mm(part, upper) for part in parts)
-    total = sum(t_mm(part, ones) for part in parts)
+    cum = sum(mm_t(lower, part) for part in parts)
+    cum_row = sum(mm(part, upper) for part in parts)
+    total = sum(mm(part, ones) for part in parts)
+    ready(0)
+    wide = bytes_ref[...].astype(f32)
+    normed = (wide * lax.rsqrt(jnp.mean(wide * wide, axis=-1, keepdims=True) + eps)).astype(bf16)
+    ready(1)
+    bc = mm(normed, wbc_ref[...]).astype(bf16)
+    bmat, cmat = bc[:, :state_n], bc[:, state_n:]
+    c_ref[...] = cmat
+    ready(2)
+    xs = mm(normed, wx_ref[...]).astype(bf16)
     last = cum[rows - 1 : rows, :]
     grow_ref[...] = jnp.exp(cum)
     tail = jnp.exp(last - cum)
@@ -73,6 +97,7 @@
     for i, piece in enumerate(pieces):
         start = heads * state_n + 16 * i
         state_ref[start : start + 16, :] = jnp.concatenate([piece, filler], axis=0).astype(bf16)
+    ready(3)
     z = mm(normed, wz_ref[...])
     gate_ref[...] = z * jax.nn.sigmoid(z)
     half = rows // 2
@@ -157,8 +182,15 @@
     place_ref[...] = jnp.where(slot == iota((count, slots), 1), 1.0, 0.0).astype(bf16)
 
 
-def attend_kernel(group, split, q_ref, all_ref, wo_ref, out_ref):
+def attend_kernel(
+    group, split, q_ref, all_ref, wo_ref, part_ref, got_ref, bytes_hbm, out_ref, enc_ref, base, sem
+):
     me = lax.axis_index("seq")
+    col = lax.axis_index("tp")
+    quarter = base.shape[1]
+    span = pl.ds(pl.multiple_of(col * quarter, 128), quarter)
+    fetch = pltpu.make_async_copy(bytes_hbm.at[:, span], base, sem)
+    fetch.start()
     ranks, count, width2 = all_ref.shape
     width = width2 // 2
     heads = width // HD
@@ -199,6 +231,11 @@
     size = wo_ref.shape[1] // split
     for q in range(split):
         out_ref[q] = mm(attended, wo_ref[:, q * size : (q + 1) * size]).astype(bf16)
+    fetch.wait()
+    summed = part_ref[col].astype(f32)
+    for d in range(1, split):
+        summed = summed + got_ref[lax.rem(col + d, split)].astype(f32)
+    enc_ref[...] = (base[...].astype(f32) + summed).astype(bf16)
 
 
 def greet(devices):
@@ -323,13 +360,22 @@
         in_specs=[VM] * len(args),
         out_specs=[VM] * len(shapes),
         scratch_shapes=scratch,
+        cost_estimate=cost(15),
         compiler_params=pltpu.CompilerParams(
             collective_id=cid, has_side_effects=True, vmem_limit_bytes=LIMIT
         ),
     )(*args)
 
 
-def rows_kernel(rows_ref, base_ref, out_ref, got, mine, ts, tr, gs, gr, own):
+def rows_kernel(
+    rows_ref, base_ref, wq, wk, wv, out_ref, vq, vk, vv, got, mine, ts, tr, gs, gr, own
+):
+    fetches = [
+        pltpu.make_async_copy(src, dst, own.at[i])
+        for i, (src, dst) in enumerate(((wq, vq), (wk, vk), (wv, vv)))
+    ]
+    for fetch in fetches:
+        fetch.start()
     me = lax.axis_index("tp")
     peers = others("tp")
     greet([{"tp": peer} for peer in peers])
@@ -348,7 +394,7 @@
     for copy in copies:
         copy.start()
     out_ref[me] = mine[...]
-    for copy in copies:
+    for copy in copies + fetches:
         copy.wait()
 
 
@@ -421,15 +467,17 @@
     cap = max(2, 2 * count // ranks)
     wide = w_q.shape[0]
     shape = jax.ShapeDtypeStruct
-    params = pltpu.CompilerParams(vmem_limit_bytes=3 * LIMIT)
-
-    def call(kernel, outs, *args):
+
+    def call(kernel, outs, *args, far=(), scratch=(), us=2, grant=3 * LIMIT):
+        specs = [HBM if i in far else VM for i in range(len(args))]
         return pl.pallas_call(
             kernel,
             out_shape=outs,
-            in_specs=[VM] * len(args),
+            in_specs=specs,
             out_specs=[VM] * len(outs),
-            compiler_params=params,
+            scratch_shapes=list(scratch),
+            cost_estimate=cost(us),
+            compiler_params=pltpu.CompilerParams(vmem_limit_bytes=grant),
         )(*args)
 
     mixed, gate, cmat, grow, state = call(
@@ -441,7 +489,11 @@
             shape((rows, heads), f32),
             shape((heads * state_n + 48, inner // heads), bf16),
         ],
-        byte_states, w_x, w_z, w_bc, log_decay,
+        byte_states, w_x, w_z, w_bc, log_decay.T,
+        far=(0, 1, 2, 3),
+        scratch=[pltpu.VMEM(a.shape, bf16) for a in (byte_states, w_x, w_z, w_bc)] + [DMA((4, 2))],
+        us=4,
+        grant=64000000,
     )
     (every,) = upward(state, cid=1)
     part, partial_rows, base = call(
@@ -454,21 +506,23 @@
         every, mixed, gate, cmat, grow, w_out, flags.reshape(1, rows), byte_states,
     )
     peers = max(split - 1, 1)
-    stretch_rows = pl.pallas_call(
+    stretch_rows, w_q, w_k, w_v = pl.pallas_call(
         rows_kernel,
-        out_shape=shape((split, count, quarter), bf16),
-        in_specs=[VM] * 2,
-        out_specs=VM,
+        out_shape=[shape((split, count, quarter), bf16)]
+        + [shape(w.shape, w.dtype) for w in (w_q, w_k, w_v)],
+        in_specs=[VM] * 2 + [HBM] * 3,
+        out_specs=[VM] * 4,
         scratch_shapes=[
             pltpu.VMEM((split, count, quarter), bf16),
             pltpu.VMEM((count, quarter), bf16),
         ]
         + [DMA((peers,))] * 4
-        + [DMA],
+        + [DMA((3,))],
+        cost_estimate=cost(10),
         compiler_params=pltpu.CompilerParams(
             collective_id=2, has_side_effects=True, vmem_limit_bytes=LIMIT
         ),
-    )(partial_rows, base)
+    )(partial_rows, base, w_q, w_k, w_v)
     queries, kv, stream, place = call(
         project_kernel,
         [
@@ -481,10 +535,12 @@
     )
     every_kv, got = upward(kv, part, cid=3)
     group = math.gcd(ranks, 8)
-    (partial_main,) = call(
+    partial_main, enc_out = call(
         functools.partial(attend_kernel, group, split),
-        [shape((split, count, wide // split), bf16)],
-        queries, every_kv, w_o,
+        [shape((split, count, wide // split), bf16), shape((rows, quarter), bf16)],
+        queries, every_kv, w_o, part, got, byte_states,
+        far=(5,),
+        scratch=[pltpu.VMEM((rows, quarter), bf16), DMA],
     )
     main_out = pl.pallas_call(
         final_kernel,
@@ -499,19 +555,13 @@
         + [DMA((peers,))] * 2
         + [DMA((max(ranks - 1, 1),))] * 2
         + [DMA((split // 2, ranks))] * 4,
+        cost_estimate=cost(20),
         compiler_params=pltpu.CompilerParams(
             collective_id=4, has_side_effects=True, vmem_limit_bytes=LIMIT
         ),
     )(partial_main, stream, place)
     main_out = main_out.reshape(ranks * cap, wide)
-    me = lax.axis_index("tp")
-    own = lax.dynamic_index_in_dim(part, me, 0, keepdims=False).astype(f32)
-    summed = own
-    for d in range(1, split):
-        peer = lax.rem(me + d, split)
-        summed = summed + lax.dynamic_index_in_dim(got, peer, 0, keepdims=False).astype(f32)
-    mine = lax.dynamic_slice_in_dim(byte_states, me * quarter, quarter, 1).astype(f32)
-    return ((mine + summed).astype(bf16), main_out)
+    return (enc_out, main_out)
 
 
 def solution(mesh):

time: 90.6 us -> 88 us (0.971)
  local copies, waits for them, and re-layouts: 9.12 us -> 3.28 us
  Pallas kernels: 78.4 us -> 83.7 us
  other arithmetic: 1.83 us -> 0 us
    unnamed x27 -> x26, local copies, waits for them, and re-layouts: 9.11 us -> 2.6 us
    pallas_call x5, Pallas kernels: 18.9 us -> 23.8 us  [the longest x4 13.4 us: call(): pl.pallas_call(kernel, out_shape=outs, in_specs=specs, out_specs=[VM] * l...]
    convert_element_type x1 -> x0, other arithmetic: 1.83 us -> none  [on_device(): return ((mine + summed).astype(bf16), main_out)]
where the time goes in v3:
time: 88 us; the launch traced here: 87.8 us
  Pallas kernels  83.7 us (95%)
  local copies, waits for them, and re-layouts  3.28 us (4%)
    pallas_call x2, Pallas kernels, upward(): pl.pallas_call(functools.partial(upward_kernel, part is not None), out_sh...  35.2 us
    pallas_call x1, Pallas kernels, on_device(): pl.pallas_call(final_kernel, out_shape=shape((ranks, cap, wide), bf16), i...  24.7 us
    pallas_call x4, Pallas kernels, call(): pl.pallas_call(kernel, out_shape=outs, in_specs=specs, out_specs=[VM] * l...  13.4 us
    pallas_call x1, Pallas kernels, on_device(): pl.pallas_call(rows_kernel, out_shape=[shape((split, count, quarter), bf1...  10.4 us
    unnamed x26, local copies, waits for them, and re-layouts  2.6 us

profile of v3, /device:TPU:0, one launch (start us, length us, event | category | flops | bytes accessed | tf_op | source)
XLA Modules:
  0.0 87.8 jit_solution(12157658458192655959)
XLA Ops:
  0.6 0.7 reshape.14.pad_ref
  1.3 0.8 copy.15.owner_ref
  2.1 6.6 %shard_map.140 = (f32[512,512]{1,0:T(8,128)}, f32[512,512]{1,0:T(8,128)}, bf16[512,128]{1,0:T(8,128)(2,1)}, f32[512,4]{1,0:T(8,128)}, bf16[560,128]{1,0:T(8,128)(2,1)}) custom-call(bf16[512,1024]{1,0:T(8,128)(2,1)} %bytes_hbm.3, bf16[1024,512]{1,0:T(8,128)(2,1)} %wx_hbm.1, bf16[1024,512]{1,0:T(8,128)(2,1)} %wz_hbm.1, bf16[1024,256]{1,0:T(8,128)(2,1)} %wbc_hbm.1, ...), custom_call_target="tpu_custom_call" | custom-call | flops 4000000000 | bytes 12000000 | tf_op jit(solution)/shard_map/pallas_call | solution.py:473
  8.7 0.0 copy-start.11
  8.7 0.9 %copy-done.11 = bf16[560,128]{1,0:T(8,128)(2,1)S(1)} copy-done((bf16[560,128]{1,0:T(8,128)(2,1)S(1)}, bf16[560,128]{1,0:T(8,128)(2,1)}, u32[]{:S(2)}) %copy-start.11) | copy-done | bytes 143384
  9.6 0.0 copy-start.4
  9.6 0.0 copy-start.5
  9.6 0.0 copy-start.6
  9.6 0.0 copy-start.7
  9.6 0.0 copy-start.8
  9.6 0.0 copy-start.9
  9.6 0.0 copy-start.10
  9.7 11.1 %shard_map.141.every_ref = bf16[8,560,128]{2,1,0:T(8,128)(2,1)S(1)} custom-call(bf16[560,128]{1,0:T(8,128)(2,1)S(1)} %copy-done.11), custom_call_target="tpu_custom_call" | custom-call | flops 15000000512 | bytes 45000000 | tf_op jit(solution)/shard_map/pallas_call | solution.py:357
  20.8 0.0 copy-done.4
  20.8 0.0 copy-done.5
  20.8 0.0 copy-done.6
  20.8 0.0 copy-done.7
  20.9 0.0 copy-done.8
  20.9 0.0 copy-done.9
  20.9 0.0 copy-done.10
  20.9 0.0 copy-start
  20.9 0.0 copy-start.1
  20.9 0.0 copy-start.2
  20.9 3.0 %shard_map.142 = (bf16[4,512,256]{2,1,0:T(8,128)(2,1)S(1)}, bf16[4,128,256]{2,1,0:T(8,128)(2,1)S(1)}, bf16[128,1024]{1,0:T(8,128)(2,1)S(1)}) custom-call(bf16[8,560,128]{2,1,0:T(8,128)(2,1)S(1)} %shard_map.141.every_ref, f32[512,512]{1,0:T(8,128)S(1)} %copy-done.7, f32[512,512]{1,0:T(8,128)S(1)} %copy-done.8, bf16[512,128]{1,0:T(8,128)(2,1)S(1)} %copy-done.10, ...), custom_call_target="tpu_custom_call" | custom-call | flops 2000000000 | bytes 6000000 | tf_op jit(solution)/shard_map/pallas_call | solution.py:473
  23.9 0.0 copy-done
  24.0 0.0 copy-done.1
  24.0 0.0 copy-done.2
  24.0 10.4 %shard_map.143 = (bf16[4,128,256]{2,1,0:T(8,128)(2,1)S(1)}, bf16[1536,384]{1,0:T(8,128)(2,1)S(1)}, bf16[1536,384]{1,0:T(8,128)(2,1)S(1)}, bf16[1536,384]{1,0:T(8,128)(2,1)S(1)}) custom-call(bf16[4,128,256]{2,1,0:T(8,128)(2,1)S(1)} %get-tuple-element.27.rows_ref, bf16[128,1024]{1,0:T(8,128)(2,1)S(1)} %get-tuple-element.28.base_ref, ...), custom_call_target="tpu_custom_call" | custom-call | flops 10000000000 | bytes 30000000 | tf_op jit(solution)/shard_map/pallas_call | solution.py:509
  34.4 1.1 %shard_map.144 = (bf16[128,384]{1,0:T(8,128)(2,1)S(1)}, bf16[128,768]{1,0:T(8,128)(2,1)S(1)}, bf16[4,128,384]{2,1,0:T(8,128)(2,1)S(1)}, bf16[128,256]{1,0:T(8,128)(2,1)S(1)}) custom-call(bf16[4,128,256]{2,1,0:T(8,128)(2,1)S(1)} %get-tuple-element.29.rows_ref, bf16[1,512]{1,0:T(2,128)(2,1)S(1)} %reshape.14.pad_ref, ...), custom_call_target="tpu_custom_call" | custom-call | flops 2000000000 | bytes 6000000 | tf_op jit(solution)/shard_map/pallas_call | solution.py:473
  35.5 0.0 copy-start.3
  35.5 24.0 %shard_map.145 = (bf16[8,128,768]{2,1,0:T(8,128)(2,1)S(1)}, bf16[4,512,256]{2,1,0:T(8,128)(2,1)S(1)}) custom-call(bf16[128,768]{1,0:T(8,128)(2,1)S(1)} %get-tuple-element.34.refs_0_, bf16[4,512,256]{2,1,0:T(8,128)(2,1)S(1)} %get-tuple-element.35.refs_1_.part_ref), custom_call_target="tpu_custom_call" | custom-call | flops 15000000512 | bytes 45000000 | tf_op jit(solution)/shard_map/pallas_call | solution.py:357
  59.5 0.0 copy-done.3
  59.5 2.7 %shard_map.146 = (bf16[4,128,384]{2,1,0:T(8,128)(2,1)S(1)}, bf16[512,256]{1,0:T(8,128)(2,1)}) custom-call(bf16[128,384]{1,0:T(8,128)(2,1)S(1)} %get-tuple-element.33.q_ref, bf16[8,128,768]{2,1,0:T(8,128)(2,1)S(1)} %get-tuple-element.36.all_ref, bf16[384,1536]{1,0:T(8,128)(2,1)S(1)} %copy-done.3, bf16[4,512,256]{2,1,0:T(8,128)(2,1)S(1)} %get-tuple-element.35.refs_1_.part_ref, ...), custom_call_target="tpu_custom_call" | custom-call | flops 2000000000 | bytes 6000000 | tf_op jit(solution)/shard_map/pallas_call | solution.py:473
  62.2 24.7 %shard_map.147 = bf16[8,32,1536]{2,1,0:T(8,128)(2,1)S(1)} custom-call(bf16[4,128,384]{2,1,0:T(8,128)(2,1)S(1)} %get-tuple-element.39.part_ref, bf16[4,128,384]{2,1,0:T(8,128)(2,1)S(1)} %get-tuple-element.40.stream_ref, bf16[128,256]{1,0:T(8,128)(2,1)S(1)} %get-tuple-element.41.place_ref), custom_call_target="tpu_custom_call" | custom-call | flops 20000000000 | bytes 60000000 | tf_op jit(solution)/shard_map/pallas_call | solution.py:545
  86.9 0.9 %copy.17 = bf16[256,1536]{1,0:T(8,128)(2,1)} copy(bf16[256,1536]{1,0:T(8,128)(2,1)S(1)} %bitcast.3) | data formatting | bytes 1572864
Async XLA Ops:
  8.7 0.9 %copy-start.11 = (bf16[560,128]{1,0:T(8,128)(2,1)S(1)}, bf16[560,128]{1,0:T(8,128)(2,1)}, u32[]{:S(2)}) copy-start(bf16[560,128]{1,0:T(8,128)(2,1)} %get-tuple-element.22.refs_0_) | copy-start | bytes 430084
  9.6 11.2 %copy-start.4 = (bf16[512,1024]{1,0:T(8,128)(2,1)S(1)}, bf16[512,1024]{1,0:T(8,128)(2,1)}, u32[]{:S(2)}) copy-start(bf16[512,1024]{1,0:T(8,128)(2,1)} %wout_ref.1) | copy-start | bytes 3145732
  9.6 11.2 %copy-start.5 = (bf16[512,1024]{1,0:T(8,128)(2,1)S(1)}, bf16[512,1024]{1,0:T(8,128)(2,1)}, u32[]{:S(2)}) copy-start(bf16[512,1024]{1,0:T(8,128)(2,1)} %bytes_hbm.3) | copy-start | bytes 3145732
  9.6 11.2 %copy-start.6 = (s32[512]{0:T(512)S(1)}, s32[512]{0:T(512)}, u32[]{:S(2)}) copy-start(s32[512]{0:T(512)} %param.14) | copy-start | bytes 6148
  9.6 11.2 %copy-start.7 = (f32[512,512]{1,0:T(8,128)S(1)}, f32[512,512]{1,0:T(8,128)}, u32[]{:S(2)}) copy-start(f32[512,512]{1,0:T(8,128)} %get-tuple-element.23.mixed_ref) | copy-start | bytes 3145732
  9.6 11.2 %copy-start.8 = (f32[512,512]{1,0:T(8,128)S(1)}, f32[512,512]{1,0:T(8,128)}, u32[]{:S(2)}) copy-start(f32[512,512]{1,0:T(8,128)} %get-tuple-element.24.gate_ref) | copy-start | bytes 3145732
  9.6 11.2 %copy-start.9 = (f32[512,4]{1,0:T(8,128)S(1)}, f32[512,4]{1,0:T(8,128)}, u32[]{:S(2)}) copy-start(f32[512,4]{1,0:T(8,128)} %get-tuple-element.26.grow_ref) | copy-start | bytes 24580
  9.6 11.2 %copy-start.10 = (bf16[512,128]{1,0:T(8,128)(2,1)S(1)}, bf16[512,128]{1,0:T(8,128)(2,1)}, u32[]{:S(2)}) copy-start(bf16[512,128]{1,0:T(8,128)(2,1)} %get-tuple-element.25.c_ref) | copy-start | bytes 393220
  20.9 3.1 %copy-start = (bf16[1536,384]{1,0:T(8,128)(2,1)S(1)}, bf16[1536,384]{1,0:T(8,128)(2,1)}, u32[]{:S(2)}) copy-start(bf16[1536,384]{1,0:T(8,128)(2,1)} %wq.1) | copy-start | bytes 3538948
  20.9 3.1 %copy-start.1 = (bf16[1536,384]{1,0:T(8,128)(2,1)S(1)}, bf16[1536,384]{1,0:T(8,128)(2,1)}, u32[]{:S(2)}) copy-start(bf16[1536,384]{1,0:T(8,128)(2,1)} %wk.1) | copy-start | bytes 3538948
  20.9 3.1 %copy-start.2 = (bf16[1536,384]{1,0:T(8,128)(2,1)S(1)}, bf16[1536,384]{1,0:T(8,128)(2,1)}, u32[]{:S(2)}) copy-start(bf16[1536,384]{1,0:T(8,128)(2,1)} %wv.1) | copy-start | bytes 3538948
  35.5 24.1 %copy-start.3 = (bf16[384,1536]{1,0:T(8,128)(2,1)S(1)}, bf16[384,1536]{1,0:T(8,128)(2,1)}, u32[]{:S(2)}) copy-start(bf16[384,1536]{1,0:T(8,128)(2,1)} %wo_ref.1) | copy-start | bytes 3538948

commit v4 on v3

--- a/solution.py
+++ b/solution.py
@@ -159,7 +159,7 @@
 
 def project_kernel(rows_ref, pad_ref, wq_ref, wk_ref, wv_ref, owner_ref, q_ref, kv_ref, stream_ref, place_ref):
     split, count, quarter = rows_ref.shape
-    pad = jnp.broadcast_to(pad_ref[...].astype(f32), (count, pad_ref.shape[1])).astype(bf16)
+    pad = jnp.broadcast_to(pad_ref[...].astype(f32).reshape(1, -1), (count, pad_ref.shape[0])).astype(bf16)
     stream = jnp.concatenate([rows_ref[q] for q in range(split)] + [pad], axis=1)
     size = stream.shape[1] // split
     for q in range(split):
@@ -170,16 +170,16 @@
     width = wk_ref.shape[1]
     kv_ref[:, :width] = mm(norm, wk_ref[...]).astype(bf16)
     kv_ref[:, width:] = mm(norm, wv_ref[...]).astype(bf16)
-    slots = place_ref.shape[1]
+    slots = place_ref.shape[0]
     owner = owner_ref[...]
     ranks = -(-lax.axis_size("seq") // 128) * 128
-    hot = jnp.where(owner == iota((count, ranks), 1), 1.0, 0.0)
-    strict = jnp.where(iota((count, count), 0) > iota((count, count), 1), 1.0, 0.0)
-    before = mm(strict.astype(bf16), hot.astype(bf16))
-    order = jnp.sum(before * hot, axis=1, keepdims=True).astype(jnp.int32)
+    hot = jnp.where(owner == iota((ranks, count), 0), 1.0, 0.0)
+    strict = jnp.where(iota((count, count), 0) < iota((count, count), 1), 1.0, 0.0)
+    before = mm(hot.astype(bf16), strict.astype(bf16))
+    order = jnp.sum(before * hot, axis=0, keepdims=True).astype(jnp.int32)
     cap = slots // lax.axis_size("seq")
     slot = owner * cap + order
-    place_ref[...] = jnp.where(slot == iota((count, slots), 1), 1.0, 0.0).astype(bf16)
+    place_ref[...] = jnp.where(slot == iota((slots, count), 0), 1.0, 0.0).astype(bf16)
 
 
 def attend_kernel(
@@ -414,7 +414,7 @@
     for peer in peers:
         total = total + got[peer].astype(f32)
     main = total.astype(bf16)
-    send[...] = t_mm(place_ref[...], main).astype(bf16).reshape(ranks, cap, size)
+    send[...] = mm(place_ref[...], main).astype(bf16).reshape(ranks, cap, size)
     copies = swap_start(send, mine, "seq", ss, sr)
     mine[seq] = send[seq]
 
@@ -529,9 +529,9 @@
             shape((count, w_q.shape[1]), bf16),
             shape((count, 2 * w_k.shape[1]), bf16),
             shape((split, count, wide // split), bf16),
-            shape((count, ranks * cap), bf16),
+            shape((ranks * cap, count), bf16),
         ],
-        stretch_rows, pad_vector.reshape(1, -1), w_q, w_k, w_v, stretch_owner,
+        stretch_rows, pad_vector, w_q, w_k, w_v, stretch_owner.reshape(1, count),
     )
     every_kv, got = upward(kv, part, cid=3)
     group = math.gcd(ranks, 8)

time: 88 us -> 86.2 us (0.980)
  local copies, waits for them, and re-layouts: 3.28 us -> 1.85 us
    unnamed x26 -> x29, local copies, waits for them, and re-layouts: 2.6 us -> 1.85 us
where the time goes in v4:
time: 86.2 us; the launch traced here: 86 us
  Pallas kernels  83.2 us (97%)
  local copies, waits for them, and re-layouts  1.85 us (2%)
  between operations  0.88 us (1%)
    pallas_call x2, Pallas kernels, upward(): pl.pallas_call(functools.partial(upward_kernel, part is not None), out_sh...  35.2 us
    pallas_call x1, Pallas kernels, on_device(): pl.pallas_call(final_kernel, out_shape=shape((ranks, cap, wide), bf16), i...  24.4 us
    pallas_call x4, Pallas kernels, call(): pl.pallas_call(kernel, out_shape=outs, in_specs=specs, out_specs=[VM] * l...  13.3 us
    pallas_call x1, Pallas kernels, on_device(): pl.pallas_call(rows_kernel, out_shape=[shape((split, count, quarter), bf1...  10.4 us
    unnamed x29, local copies, waits for them, and re-layouts  1.85 us

profile of v4, /device:TPU:0, one launch (start us, length us, event | category | flops | bytes accessed | tf_op | source)
XLA Modules:
  0.0 86.0 jit_solution(10804017684298886115)
XLA Ops:
  0.6 6.6 %shard_map.140 = (f32[512,512]{1,0:T(8,128)}, f32[512,512]{1,0:T(8,128)}, bf16[512,128]{1,0:T(8,128)(2,1)}, f32[512,4]{1,0:T(8,128)}, bf16[560,128]{1,0:T(8,128)(2,1)}) custom-call(bf16[512,1024]{1,0:T(8,128)(2,1)} %bytes_hbm.3, bf16[1024,512]{1,0:T(8,128)(2,1)} %wx_hbm.1, bf16[1024,512]{1,0:T(8,128)(2,1)} %wz_hbm.1, bf16[1024,256]{1,0:T(8,128)(2,1)} %wbc_hbm.1, ...), custom_call_target="tpu_custom_call" | custom-call | flops 4000000000 | bytes 12000000 | tf_op jit(solution)/shard_map/pallas_call | solution.py:473
  7.3 0.0 copy-start.13
  7.3 0.9 %copy-done.13 = bf16[560,128]{1,0:T(8,128)(2,1)S(1)} copy-done((bf16[560,128]{1,0:T(8,128)(2,1)S(1)}, bf16[560,128]{1,0:T(8,128)(2,1)}, u32[]{:S(2)}) %copy-start.13) | copy-done | bytes 143384
  8.2 0.0 copy-start.4
  8.2 0.0 copy-start.5
  8.2 0.0 copy-start.6
  8.2 0.0 copy-start.9
  8.2 0.0 copy-start.10
  8.2 0.0 copy-start.11
  8.2 0.0 copy-start.12
  8.2 11.1 %shard_map.141.every_ref = bf16[8,560,128]{2,1,0:T(8,128)(2,1)S(1)} custom-call(bf16[560,128]{1,0:T(8,128)(2,1)S(1)} %copy-done.13), custom_call_target="tpu_custom_call" | custom-call | flops 15000000512 | bytes 45000000 | tf_op jit(solution)/shard_map/pallas_call | solution.py:357
  19.4 0.0 copy-done.4
  19.4 0.0 copy-done.5
  19.4 0.0 copy-done.6
  19.4 0.0 copy-done.9
  19.4 0.0 copy-done.10
  19.4 0.0 copy-done.11
  19.4 0.0 copy-done.12
  19.4 0.0 copy-start
  19.4 0.0 copy-start.1
  19.5 0.0 copy-start.2
  19.5 3.0 %shard_map.142 = (bf16[4,512,256]{2,1,0:T(8,128)(2,1)S(1)}, bf16[4,128,256]{2,1,0:T(8,128)(2,1)S(1)}, bf16[128,1024]{1,0:T(8,128)(2,1)S(1)}) custom-call(bf16[8,560,128]{2,1,0:T(8,128)(2,1)S(1)} %shard_map.141.every_ref, f32[512,512]{1,0:T(8,128)S(1)} %copy-done.9, f32[512,512]{1,0:T(8,128)S(1)} %copy-done.10, bf16[512,128]{1,0:T(8,128)(2,1)S(1)} %copy-done.12, ...), custom_call_target="tpu_custom_call" | custom-call | flops 2000000000 | bytes 6000000 | tf_op jit(solution)/shard_map/pallas_call | solution.py:473
  22.5 0.0 copy-done
  22.5 0.0 copy-done.1
  22.5 0.0 copy-done.2
  22.5 0.0 copy-start.7
  22.5 0.0 copy-start.8
  22.5 10.4 %shard_map.143 = (bf16[4,128,256]{2,1,0:T(8,128)(2,1)S(1)}, bf16[1536,384]{1,0:T(8,128)(2,1)S(1)}, bf16[1536,384]{1,0:T(8,128)(2,1)S(1)}, bf16[1536,384]{1,0:T(8,128)(2,1)S(1)}) custom-call(bf16[4,128,256]{2,1,0:T(8,128)(2,1)S(1)} %get-tuple-element.27.rows_ref, bf16[128,1024]{1,0:T(8,128)(2,1)S(1)} %get-tuple-element.28.base_ref, ...), custom_call_target="tpu_custom_call" | custom-call | flops 10000000000 | bytes 30000000 | tf_op jit(solution)/shard_map/pallas_call | solution.py:509
  32.9 0.0 copy-done.7
  32.9 0.0 copy-done.8
  33.0 1.0 %shard_map.144 = (bf16[128,384]{1,0:T(8,128)(2,1)S(1)}, bf16[128,768]{1,0:T(8,128)(2,1)S(1)}, bf16[4,128,384]{2,1,0:T(8,128)(2,1)S(1)}, bf16[256,128]{1,0:T(8,128)(2,1)S(1)}) custom-call(bf16[4,128,256]{2,1,0:T(8,128)(2,1)S(1)} %get-tuple-element.29.rows_ref, bf16[512]{0:T(512)(128)(2,1)S(1)} %copy-done.7, bf16[1536,384]{1,0:T(8,128)(2,1)S(1)} %get-tuple-element.30.wq_ref, ...), custom_call_target="tpu_custom_call" | custom-call | flops 2000000000 | bytes 6000000 | tf_op jit(solution)/shard_map/pallas_call | solution.py:473
  33.9 0.0 copy-start.3
  33.9 24.0 %shard_map.145 = (bf16[8,128,768]{2,1,0:T(8,128)(2,1)S(1)}, bf16[4,512,256]{2,1,0:T(8,128)(2,1)S(1)}) custom-call(bf16[128,768]{1,0:T(8,128)(2,1)S(1)} %get-tuple-element.34.refs_0_, bf16[4,512,256]{2,1,0:T(8,128)(2,1)S(1)} %get-tuple-element.35.refs_1_.part_ref), custom_call_target="tpu_custom_call" | custom-call | flops 15000000512 | bytes 45000000 | tf_op jit(solution)/shard_map/pallas_call | solution.py:357
  58.0 0.0 copy-done.3
  58.0 2.7 %shard_map.146 = (bf16[4,128,384]{2,1,0:T(8,128)(2,1)S(1)}, bf16[512,256]{1,0:T(8,128)(2,1)}) custom-call(bf16[128,384]{1,0:T(8,128)(2,1)S(1)} %get-tuple-element.33.q_ref, bf16[8,128,768]{2,1,0:T(8,128)(2,1)S(1)} %get-tuple-element.36.all_ref, bf16[384,1536]{1,0:T(8,128)(2,1)S(1)} %copy-done.3, bf16[4,512,256]{2,1,0:T(8,128)(2,1)S(1)} %get-tuple-element.35.refs_1_.part_ref, ...), custom_call_target="tpu_custom_call" | custom-call | flops 2000000000 | bytes 6000000 | tf_op jit(solution)/shard_map/pallas_call | solution.py:473
  60.7 24.4 %shard_map.147 = bf16[8,32,1536]{2,1,0:T(8,128)(2,1)S(1)} custom-call(bf16[4,128,384]{2,1,0:T(8,128)(2,1)S(1)} %get-tuple-element.39.part_ref, bf16[4,128,384]{2,1,0:T(8,128)(2,1)S(1)} %get-tuple-element.40.stream_ref, bf16[256,128]{1,0:T(8,128)(2,1)S(1)} %get-tuple-element.41.place_ref), custom_call_target="tpu_custom_call" | custom-call | flops 20000000000 | bytes 60000000 | tf_op jit(solution)/shard_map/pallas_call | solution.py:545
  85.1 0.9 %copy.16 = bf16[256,1536]{1,0:T(8,128)(2,1)} copy(bf16[256,1536]{1,0:T(8,128)(2,1)S(1)} %bitcast.4) | data formatting | bytes 1572864
Async XLA Ops:
  7.3 0.9 %copy-start.13 = (bf16[560,128]{1,0:T(8,128)(2,1)S(1)}, bf16[560,128]{1,0:T(8,128)(2,1)}, u32[]{:S(2)}) copy-start(bf16[560,128]{1,0:T(8,128)(2,1)} %get-tuple-element.22.refs_0_) | copy-start | bytes 430084
  8.2 11.2 %copy-start.4 = (bf16[512,1024]{1,0:T(8,128)(2,1)S(1)}, bf16[512,1024]{1,0:T(8,128)(2,1)}, u32[]{:S(2)}) copy-start(bf16[512,1024]{1,0:T(8,128)(2,1)} %wout_ref.1) | copy-start | bytes 3145732
  8.2 11.2 %copy-start.5 = (bf16[512,1024]{1,0:T(8,128)(2,1)S(1)}, bf16[512,1024]{1,0:T(8,128)(2,1)}, u32[]{:S(2)}) copy-start(bf16[512,1024]{1,0:T(8,128)(2,1)} %bytes_hbm.3) | copy-start | bytes 3145732
  8.2 11.2 %copy-start.6 = (s32[512]{0:T(512)S(1)}, s32[512]{0:T(512)}, u32[]{:S(2)}) copy-start(s32[512]{0:T(512)} %param.14) | copy-start | bytes 6148
  8.2 11.2 %copy-start.9 = (f32[512,512]{1,0:T(8,128)S(1)}, f32[512,512]{1,0:T(8,128)}, u32[]{:S(2)}) copy-start(f32[512,512]{1,0:T(8,128)} %get-tuple-element.23.mixed_ref) | copy-start | bytes 3145732
  8.2 11.2 %copy-start.10 = (f32[512,512]{1,0:T(8,128)S(1)}, f32[512,512]{1,0:T(8,128)}, u32[]{:S(2)}) copy-start(f32[512,512]{1,0:T(8,128)} %get-tuple-element.24.gate_ref) | copy-start | bytes 3145732
  8.2 11.2 %copy-start.11 = (f32[512,4]{1,0:T(8,128)S(1)}, f32[512,4]{1,0:T(8,128)}, u32[]{:S(2)}) copy-start(f32[512,4]{1,0:T(8,128)} %get-tuple-element.26.grow_ref) | copy-start | bytes 24580
  8.2 11.2 %copy-start.12 = (bf16[512,128]{1,0:T(8,128)(2,1)S(1)}, bf16[512,128]{1,0:T(8,128)(2,1)}, u32[]{:S(2)}) copy-start(bf16[512,128]{1,0:T(8,128)(2,1)} %get-tuple-element.25.c_ref) | copy-start | bytes 393220
  19.4 3.1 %copy-start = (bf16[1536,384]{1,0:T(8,128)(2,1)S(1)}, bf16[1536,384]{1,0:T(8,128)(2,1)}, u32[]{:S(2)}) copy-start(bf16[1536,384]{1,0:T(8,128)(2,1)} %wq.1) | copy-start | bytes 3538948
  19.4 3.1 %copy-start.1 = (bf16[1536,384]{1,0:T(8,128)(2,1)S(1)}, bf16[1536,384]{1,0:T(8,128)(2,1)}, u32[]{:S(2)}) copy-start(bf16[1536,384]{1,0:T(8,128)(2,1)} %wk.1) | copy-start | bytes 3538948
  19.5 3.1 %copy-start.2 = (bf16[1536,384]{1,0:T(8,128)(2,1)S(1)}, bf16[1536,384]{1,0:T(8,128)(2,1)}, u32[]{:S(2)}) copy-start(bf16[1536,384]{1,0:T(8,128)(2,1)} %wv.1) | copy-start | bytes 3538948
  22.5 10.4 %copy-start.7 = (bf16[512]{0:T(512)(128)(2,1)S(1)}, bf16[512]{0:T(512)(128)(2,1)}, u32[]{:S(2)}) copy-start(bf16[512]{0:T(512)(128)(2,1)} %pad_ref.1) | copy-start | bytes 3076
  22.5 10.4 %copy-start.8 = (s32[128,1]{0,1:T(1,128)S(1)}, s32[128,1]{0,1:T(1,128)}, u32[]{:S(2)}) copy-start(s32[128,1]{0,1:T(1,128)} %param.15) | copy-start | bytes 1540
  33.9 24.1 %copy-start.3 = (bf16[384,1536]{1,0:T(8,128)(2,1)S(1)}, bf16[384,1536]{1,0:T(8,128)(2,1)}, u32[]{:S(2)}) copy-start(bf16[384,1536]{1,0:T(8,128)(2,1)} %wo_ref.1) | copy-start | bytes 3538948
